TPU v7x, 256 devices: a whole 4x4x8 slice. The times are simulated.
256 devices in a mesh: rep: 16 (over x, y_hi, core), hid: 16 (over y_lo, z).
Axes of the slice: x: 4, y: 4 (y_hi: 2, y_lo: 2; y = y_hi * 2 + y_lo), z: 8, core: 2. Of those that a mesh axis runs over, the one named last changes fastest.
Arguments:
- tokens: bfloat16 [2, 8192, 1152], P(None, ('rep', 'hid')), may hold values from -6 to 6
- targets: bfloat16 [2, 8192, 1152], P(None, ('rep', 'hid')), may hold values from -6 to 6
- w_gate: float32 [16, 6912, 1152], P('rep', 'hid'), may hold values from -6 to 6
- w_up: float32 [16, 6912, 1152], P('rep', 'hid'), may hold values from -6 to 6
- w_down: float32 [16, 6912, 1152], P('rep', 'hid'), may hold values from -6 to 6
Outputs:
- new_gate: float32 [16, 6912, 1152], P('rep', 'hid')
- new_up: float32 [16, 6912, 1152], P('rep', 'hid')
- new_down: float32 [16, 6912, 1152], P('rep', 'hid')
All inputs are finite; a program needn't handle non-finite values.
Results may differ from a plain program's by a relative error of at most 0.0086.
Values may be sent and summed in bfloat16 or wider, within the bound.
No kernel may reach another device: no remote copies, remote signals or barrier semaphores. Data moves between devices by JAX's collectives and lax.ppermute only.
A program may use at most 128 MiB of HBM per device.

v0:
```python
import functools

import jax
import jax.numpy as jnp
from jax import lax
from jax.experimental import pallas as pl
from jax.experimental.pallas import tpu as pltpu
from jax.sharding import PartitionSpec as P

LEARNING_RATE = 0.5
SQRT_2_PI = 0.7978845608028654
CUBIC = 0.044715
LIMIT = 12
UPDATE_LIMIT = 14
BF16, F32 = jnp.bfloat16, jnp.float32


def dot_nt(left, right):
    return lax.dot_general(left, right, (((1,), (1,)), ((), ())), preferred_element_type=F32)


def dot_nn(left, right):
    return lax.dot_general(left, right, (((1,), (0,)), ((), ())), preferred_element_type=F32)


def gelu_and_slope(value):
    inner = SQRT_2_PI * (value + CUBIC * value * value * value)
    tanh = jnp.tanh(inner)
    half = 0.5 * (1.0 + tanh)
    slope = half + 0.5 * value * (1.0 - tanh * tanh) * SQRT_2_PI * (1.0 + 3.0 * CUBIC * value * value)
    return value * half, slope


VMEM_SPEC = pl.BlockSpec(memory_space=pltpu.VMEM)
SMEM_SPEC = pl.BlockSpec(memory_space=pltpu.SMEM)
HBM_SPEC = pl.BlockSpec(memory_space=pltpu.HBM)


def kernel_call(body, out_shape, args, flops, limit, scratch=(), in_specs=None, out_specs=None, alias=None):
    size = sum(v.size * v.dtype.itemsize for v in args)
    size += sum(v.size * v.dtype.itemsize for v in out_shape)
    return pl.pallas_call(
        body,
        out_shape=out_shape,
        in_specs=[VMEM_SPEC] * len(args) if in_specs is None else in_specs,
        out_specs=[VMEM_SPEC] * len(out_shape) if out_specs is None else out_specs,
        scratch_shapes=list(scratch),
        cost_estimate=pl.CostEstimate(flops=flops, bytes_accessed=size, transcendentals=0),
        compiler_params=pltpu.CompilerParams(vmem_limit_bytes=limit * 2**20),
        input_output_aliases=alias or {},
    )(*args)


def pieces(k, pair, paired, total):
    if paired:
        return ((k * pair, 0, pair),)
    half = pair // 2
    return ((k * half, 0, half), (total // 2 + k * half, half, half))


def spread(refs, target, pair, paired):
    total = target.shape[0]
    k = 0
    for ref in refs:
        for i in range(ref.shape[0] // pair):
            for start, offset, size in pieces(k, pair, paired, total):
                target[start : start + size, :] = ref[i * pair + offset : i * pair + offset + size, :]
            k += 1


COLUMNS = 384
TOKENS = 256
UNITS = 48
PART = 16


def forward_into(x, weights, saved, scale_model):
    act_ref, slope_ref, hidden_ref = saved

    @pl.loop(0, x.shape[0] // TOKENS)
    def _(step):
        start = pl.multiple_of(step * TOKENS, TOKENS)
        here = pl.ds(start, TOKENS)
        batch = x[here, :]
        gate = dot_nt(weights[0], batch) * scale_model
        up = dot_nt(weights[1], batch) * scale_model
        act, slope = gelu_and_slope(gate)
        act_ref[:, here] = act
        slope_ref[:, here] = slope * up
        hidden_ref[:, here] = (act * up).astype(BF16)


def partial_into(hidden, down, refs, pair, paired, turned):
    total = hidden.shape[1]
    turned[...] = hidden[...].T

    @pl.loop(0, down.shape[1] // COLUMNS)
    def _(step):
        here = pl.ds(pl.multiple_of(step * COLUMNS, COLUMNS), COLUMNS)
        part = dot_nn(turned[...], down[:, here]).astype(BF16)
        k = 0
        for ref in refs:
            for i in range(ref.shape[0] // pair):
                for start, offset, size in pieces(k, pair, paired, total):
                    ref[i * pair + offset : i * pair + offset + size, here] = part[
                        start : start + size
                    ]
                k += 1


def each_part(total, size, body):
    @pl.loop(0, total // size)
    def _(step):
        body(pl.multiple_of(step * size, size))


def cast_body(gate, up, down, stacked, halves):
    def one(start):
        here = pl.ds(start, UNITS)
        for i, ref in enumerate((gate, up, down)):
            stacked[i, here, :] = ref[here, :]
            halves[i, here, :] = ref[here, :].astype(BF16)

    each_part(gate.shape[0], UNITS, one)


def mean_body(mine, near, base):
    for i in range(3):

        @pl.loop(0, mine.shape[1] // UNITS)
        def _(step):
            here = pl.ds(pl.multiple_of(step * UNITS, UNITS), UNITS)
            base[i, here, :] = (mine[i, here, :] + near[i, here, :]) * 0.5


def first_forward_body(pair, scale_model, *refs):
    blocks, targets, halves = refs[:6], refs[6], refs[7]
    x, column, act, slope, hidden = refs[8:13]
    partials, turned = refs[13:19], refs[19]
    rows = pair // 2
    size = pair + rows
    k = 0
    for ref in blocks:
        for i in range(ref.shape[0] // size):
            x[k * pair : (k + 1) * pair, :] = ref[i * size : i * size + pair, :]
            column[k * rows : (k + 1) * rows, :] = ref[i * size + pair : (i + 1) * size, :]
            k += 1
    column[k * rows : (k + 1) * rows, :] = targets[0]
    column[(k + 1) * rows :, :] = targets[1]
    forward_into(x, halves, (act, slope, hidden), scale_model)
    partial_into(hidden, halves.at[2], partials, pair, True, turned)


def gradients(residual, x, act, slope, hidden, down, scales, saved, store, tight):
    scale_model, scale_hidden = scales

    @pl.loop(0, x.shape[0] // TOKENS)
    def _(step):
        here = pl.ds(pl.multiple_of(step * TOKENS, TOKENS), TOKENS)
        hidden_grad = dot_nt(down[...], residual[here, :]) * scale_hidden
        saved[0, :, here] = (hidden_grad * slope[:, here]).astype(BF16)
        saved[1, :, here] = (hidden_grad * act[:, here]).astype(BF16)

    @pl.loop(0, x.shape[1] // COLUMNS)
    def _(step):
        here = pl.ds(pl.multiple_of(step * COLUMNS, COLUMNS), COLUMNS)
        store(2, step, here, dot_nn(hidden[...], residual[:, here]) * scale_hidden)

        def one(i):
            store(i, step, here, dot_nn(saved[i], x[:, here]) * scale_model)

        if tight:
            pl.loop(0, 2)(one)
        else:
            one(0)
            one(1)


def first_backward_body(pair, scales, *refs):
    blocks = refs[:6]
    x, act, slope, hidden, halves, grads, residual, saved = refs[6:]
    spread(blocks, residual, pair, True)

    def store(i, step, columns, value):
        grads[i, :, columns] = value.astype(BF16)

    gradients(residual, x, act, slope, hidden, halves.at[2], scales, saved, store, True)


def update_forward_body(pair, scale_model, *refs):
    core, base, grads, near_grads, x = refs[:5]
    kept, sent_in, sent_out = refs[5:10], refs[10], refs[11]
    partials, halves, turned = refs[12:18], refs[18], refs[19]
    size = sent_in.shape[0] * 2 // 3
    offset = core[0] * (halves.shape[1] - size)
    weights, act, slope, hidden, down = kept

    for i in range(3):

        @pl.loop(0, base.shape[1] // UNITS)
        def _(step):
            here = pl.ds(pl.multiple_of(step * UNITS, UNITS), UNITS)
            moved = grads[i, here, :].astype(F32) + near_grads[i, here, :].astype(F32)
            value = base[i, here, :] - (LEARNING_RATE * 0.5) * moved
            weights[i, here, :] = value
            halves[i, here, :] = value.astype(BF16)

    forward_into(x, halves, (act, slope, hidden), scale_model)
    partial_into(hidden, halves.at[2], partials, pair, False, turned)

    def keep(start):
        down[pl.ds(start, UNITS), :] = halves[2, pl.ds(start, UNITS), :]

    def send(start):
        source = pl.ds(pl.multiple_of(offset + start, PART), PART)
        sent_in[pl.ds(start, PART), :] = halves[0, source, :]
        sent_out[pl.ds(pl.multiple_of(size // 2 + start, PART), PART), :] = halves[2, source, :]

    def send_half(start):
        source = pl.ds(pl.multiple_of(offset + start, PART), PART)
        sent_in[pl.ds(pl.multiple_of(size + start, PART), PART), :] = halves[1, source, :]
        source = pl.ds(pl.multiple_of(offset + size // 2 + start, PART), PART)
        sent_out[pl.ds(start, PART), :] = halves[1, source, :]

    each_part(down.shape[0], UNITS, keep)
    each_part(size, PART, send)
    each_part(size // 2, PART, send_half)


def far_forward_body(scale_model, core, x, direct, beside, weights, act, slope, hidden):
    size = direct.shape[0] // 3
    last = weights.shape[1] - size
    first = core[0] * last

    def place(start):
        for i in range(3):
            source = pl.ds(pl.multiple_of(i * size + start, PART), PART)
            weights[i, pl.ds(pl.multiple_of(first + start, PART), PART), :] = direct[source, :]
            weights[i, pl.ds(pl.multiple_of(last - first + start, PART), PART), :] = beside[source, :]

    each_part(size, PART, place)
    forward_into(x, weights, (act, slope, hidden), scale_model)


def join_body(direct_in, direct_out, joined):
    def one(start):
        here = pl.ds(start, PART)
        joined[here, :] = direct_in[here, :]
        joined[pl.ds(pl.multiple_of(direct_in.shape[0] + start, PART), PART), :] = direct_out[here, :]

    each_part(direct_in.shape[0], PART, one)


def own_backward_body(pair, scales, *refs):
    blocks = refs[:6]
    x, act, slope, hidden, down, weights, total, residual, saved = refs[6:]
    spread(blocks, residual, pair, False)

    def store(i, step, columns, value):
        total[i, :, columns] = weights[i, :, columns] * 0.5 - (LEARNING_RATE * 0.5) * value

    gradients(residual, x, act, slope, hidden, down, scales, saved, store, True)


def last_body(pair, scales, *refs):
    blocks = refs[:6]
    x, act, slope, hidden, far, total, out_gate, out_up, out_down, residual, staged, sems, saved = refs[6:]
    outs = (out_gate, out_up, out_down)
    spread(blocks, residual, pair, False)

    def out_copy(i, step, columns):
        return pltpu.make_async_copy(
            staged.at[i, :, columns], outs[i].at[0, :, columns], sems.at[i, step]
        )

    def store(i, step, columns, value):
        mean = total[i, :, columns] + far[i, :, columns].astype(F32) * 0.5
        staged[i, :, columns] = mean - (LEARNING_RATE * 0.5) * value
        out_copy(i, step, columns).start()

    gradients(residual, x, act, slope, hidden, far.at[2], scales, saved, store, False)
    for i in (2, 0, 1):
        for step in range(x.shape[1] // COLUMNS):
            out_copy(i, step, slice(step * COLUMNS, (step + 1) * COLUMNS)).wait()


def local(tokens, targets, w_gate, w_up, w_down, *, n_rep, n_z, hidden_units):
    n_hid = 2 * n_z
    rows, width = tokens.shape[1], tokens.shape[2]
    pair = 2 * rows
    scale_model = float(width) ** (-0.5)
    scale_hidden = float(hidden_units) ** (-0.5)

    def along_z(value, shift):
        pairs = [(h, (h // n_z) * n_z + (h % n_z + shift) % n_z) for h in range(n_hid)]
        return lax.ppermute(value, "hid", pairs)

    def across_y(value):
        return lax.ppermute(value, "hid", [(h, h ^ n_z) for h in range(n_hid)])

    def with_replica(value, mask):
        return lax.ppermute(value, "rep", [(r, r ^ mask) for r in range(n_rep)])

    def two_along(value, sign):
        pairs = []
        for r in range(n_rep):
            step = sign * (n_z // 4) if r % 2 == 0 else -sign * (n_z // 4)
            for h in range(n_hid):
                to = (h // n_z) * n_z + (h % n_z + step) % n_z
                pairs.append((r * n_hid + h, r * n_hid + to))
        return lax.ppermute(value, ("rep", "hid"), pairs)

    def gather_far(block):
        return two_along(block, 1), two_along(block, -1)

    def gather_near(block, ahead, behind):
        across = two_along(ahead, 1)
        both = jnp.concatenate([ahead, behind], axis=0)
        left, right = along_z(both, 1), along_z(both, -1)
        return [block, ahead, behind, across, left, right]

    def gather_z(block):
        return gather_near(block, *gather_far(block))

    def reduce_z(partials):
        own, ahead, behind, across, left, right = partials
        own, ahead, behind = (v.astype(F32) for v in (own, ahead, behind))
        across = two_along(across, -1)
        left, right = along_z(left, -1), along_z(right, 1)
        ahead = ahead + left[:pair].astype(F32) + right[:pair].astype(F32) + across.astype(F32)
        behind = behind + left[pair:].astype(F32) + right[pair:].astype(F32)
        ahead, behind = two_along(ahead.astype(BF16), -1), two_along(behind.astype(BF16), 1)
        total = own + ahead.astype(F32) + behind.astype(F32)
        other = across_y(total.astype(BF16)).astype(F32)
        return total + jnp.concatenate([other[rows:], other[:rows]], axis=0)

    def residual_of(partials, target):
        output = reduce_z(partials) * scale_hidden
        return (output - target.astype(F32)).astype(BF16)

    units = w_gate.shape[1]
    count = n_z * pair
    product = 2 * units * count * width
    scales = (scale_model, scale_hidden)

    def arr(shape, dtype):
        return jax.ShapeDtypeStruct(shape, dtype)

    stack_f32, stack_bf16 = arr((3, units, width), F32), arr((3, units, width), BF16)
    acts = [arr((units, count), F32), arr((units, count), F32), arr((units, count), BF16)]
    travel = [arr((pair, width), BF16)] * 4 + [arr((2 * pair, width), BF16)] * 2
    tokens_shape = arr((count, width), BF16)
    grad_scratch = pltpu.VMEM((2, units, count), BF16)
    residual_scratch = pltpu.VMEM((count, width), BF16)
    turned_scratch = pltpu.VMEM((count, units), BF16)

    first = jnp.concatenate([tokens[0], across_y(tokens[0]), tokens[1]], axis=0)
    mine, halves = kernel_call(
        cast_body, [stack_f32, stack_bf16], (w_gate[0], w_up[0], w_down[0]), 0, LIMIT
    )
    near = with_replica(mine, 1)
    blocks = gather_z(first)

    x0, column, act, slope, hidden, *partials = kernel_call(
        functools.partial(first_forward_body, pair, scale_model),
        [tokens_shape, arr((n_z * rows + pair, width), BF16), *acts, *travel],
        (*blocks, targets, halves),
        3 * product,
        LIMIT,
        (turned_scratch,),
    )
    beside = across_y(column)
    half = n_z * rows
    x1 = jnp.concatenate([column[:half], beside[:half]], axis=0)
    target0, target1 = (
        jnp.concatenate([targets[i], beside[half + i * rows : half + (i + 1) * rows]], axis=0)
        for i in range(2)
    )

    blocks = gather_z(residual_of(partials, target0))
    x1_far = with_replica(x1, 2)
    (grads,) = kernel_call(
        functools.partial(first_backward_body, pair, scales),
        [stack_bf16],
        (*blocks, x0, act, slope, hidden, halves),
        4 * product,
        LIMIT,
        (residual_scratch, grad_scratch),
    )
    near_grads = with_replica(grads, 1)

    (base,) = kernel_call(mean_body, [stack_f32], (mine, near), 0, UPDATE_LIMIT)

    core = (lax.axis_index("rep") % 2).astype(jnp.int32).reshape(1)
    cut = -(-units // 32) * 16
    weights, act, slope, hidden, down, sent_in, sent_out, *partials = kernel_call(
        functools.partial(update_forward_body, pair, scale_model),
        [
            stack_f32,
            *acts,
            arr((units, width), BF16),
            arr((cut * 3 // 2, width), BF16),
            arr((cut * 3 // 2, width), BF16),
            *travel,
        ],
        (core, base, grads, near_grads, x1),
        3 * product,
        UPDATE_LIMIT,
        (
            pltpu.VMEM((3, units, width), BF16),
            turned_scratch,
        ),
        [SMEM_SPEC] + [VMEM_SPEC] * 4,
    )
    direct_in = with_replica(sent_in, 2)
    direct_out = with_replica(sent_out, 2)
    (direct,) = kernel_call(
        join_body, [arr((3 * cut, width), BF16)], (direct_in, direct_out), 0, 12
    )
    passed = with_replica(direct, 1)

    residual = residual_of(partials, target1)
    residual_far = with_replica(residual, 2)
    blocks = gather_z(residual)
    far_blocks = gather_z(residual_far)
    (total,) = kernel_call(
        functools.partial(own_backward_body, pair, scales),
        [stack_f32],
        (*blocks, x1, act, slope, hidden, down, weights),
        4 * product,
        LIMIT,
        (residual_scratch, grad_scratch),
    )
    far, act, slope, hidden = kernel_call(
        functools.partial(far_forward_body, scale_model),
        [stack_bf16, *acts],
        (core, x1_far, direct, passed),
        2 * product,
        LIMIT,
        (),
        [SMEM_SPEC] + [VMEM_SPEC] * 3,
    )
    return kernel_call(
        functools.partial(last_body, pair, scales),
        [arr((1, units, width), F32)] * 3,
        (*far_blocks, x1_far, act, slope, hidden, far, total),
        4 * product,
        LIMIT,
        (
            residual_scratch,
            pltpu.VMEM((3, units, width), F32),
            pltpu.SemaphoreType.DMA((3, width // COLUMNS)),
            grad_scratch,
        ),
        None,
        [pl.BlockSpec(memory_space=pl.ANY)] * 3,
    )


def solution(mesh):
    n_rep, n_hid = mesh.shape["rep"], mesh.shape["hid"]
    hid_spec = P("rep", "hid", None)
    token_spec = P(None, ("rep", "hid"), None)

    def whole(tokens, targets, w_gate, w_up, w_down):
        def body(*args):
            return local(*args, n_rep=n_rep, n_z=n_hid // 2, hidden_units=w_gate.shape[1])

        return jax.shard_map(
            body,
            mesh=mesh,
            in_specs=(token_spec, token_spec, hid_spec, hid_spec, hid_spec),
            out_specs=(hid_spec, hid_spec, hid_spec),
            check_vma=False,
        )(tokens, targets, w_gate, w_up, w_down)

    return whole
```

profile of v0, /device:TPU:2, one launch (start us, length us, event | category | flops | bytes accessed | tf_op | source)
XLA Modules:
  0.0 240.4 jit_solution(12522990326898461283)
XLA Ops:
  0.6 0.9 slice_bitcast_fusion.3
  1.6 1.7 collective-permute-start.1
  3.2 2.8 %collective-permute-done.1 = bf16[32,1152]{1,0:T(8,128)(2,1)S(1)} collective-permute-done((bf16[32,1152]{1,0:T(8,128)(2,1)S(1)}, bf16[32,1152]{1,0:T(8,128)(2,1)S(1)}, u32[]{:S(2)}, u32[]{:S(2)}) %collective-permute-start.1) | collective-permute-done | bytes 73760 | tf_op jit(solution)/shard_map/ppermute | solution.py:299
  6.0 3.3 %collective-permute-start.2 = (bf16[96,1152]{1,0:T(8,128)(2,1)S(1)}, bf16[96,1152]{1,0:T(8,128)(2,1)S(1)}, u32[]{:S(2)}, u32[]{:S(2)}) collective-permute-start(bf16[96,1152]{1,0:T(8,128)(2,1)S(1)} %pad_maximum_fusion.1.refs_0_), channel_id=1, source_target_pairs={{0,2},{1,3},{2,4},{3,5},{4,6},{5,7},{6,0},{7,1},{8,10},{9,11},{10,... | collective-permute-start | bytes 663560 | tf_op jit(solution)/shard_map/ppermute | solution.py:311
  9.4 3.1 %collective-permute-start.3 = (bf16[96,1152]{1,0:T(8,128)(2,1)S(1)}, bf16[96,1152]{1,0:T(8,128)(2,1)S(1)}, u32[]{:S(2)}, u32[]{:S(2)}) collective-permute-start(bf16[96,1152]{1,0:T(8,128)(2,1)S(1)} %pad_maximum_fusion.1.refs_0_), channel_id=1, source_target_pairs={{0,6},{1,7},{2,0},{3,1},{4,2},{5,3},{6,4},{7,5},{8,14},{9,15},{10,... | collective-permute-start | bytes 663560 | tf_op jit(solution)/shard_map/ppermute | solution.py:311
  12.5 6.0 %collective-permute-done.2.refs_1_ = bf16[96,1152]{1,0:T(8,128)(2,1)S(1)} collective-permute-done((bf16[96,1152]{1,0:T(8,128)(2,1)S(1)}, bf16[96,1152]{1,0:T(8,128)(2,1)S(1)}, u32[]{:S(2)}, u32[]{:S(2)}) %collective-permute-start.2) | collective-permute-done | bytes 221216 | tf_op jit(solution)/shard_map/ppermute | solution.py:311
  18.5 2.2 collective-permute-done.3.refs_2_
  20.7 3.2 %collective-permute-start.5 = (bf16[192,1152]{1,0:T(8,128)(2,1)S(1)}, bf16[192,1152]{1,0:T(8,128)(2,1)S(1)}, u32[]{:S(2)}, u32[]{:S(2)}) collective-permute-start(bf16[192,1152]{1,0:T(8,128)(2,1)S(1)} %constant_dynamic-update-slice_fusion), channel_id=1, source_target_pairs={{0,1},{1,2},{2,3},{3,4},{4,5},{5,6},{6,7},{7,0},{8,9},{9,10},{10,1... | collective-permute-start | bytes 1327112 | tf_op jit(solution)/shard_map/ppermute | solution.py:296
  23.9 1.1 collective-permute-start.6
  25.0 1.2 collective-permute-start.4
  26.2 1.6 copy-done
  27.8 1.6 copy-done.1
  29.3 1.6 copy-done.2
  30.9 3.2 %shard_map.76 = (f32[3,432,1152]{2,1,0:T(8,128)}, bf16[3,432,1152]{2,1,0:T(8,128)(2,1)S(1)}) custom-call(f32[432,1152]{1,0:T(8,128)S(1)} %bitcast.12, f32[432,1152]{1,0:T(8,128)S(1)} %bitcast.13, f32[432,1152]{1,0:T(8,128)S(1)} %bitcast.14), custom_call_target="tpu_custom_call" | custom-call | bytes 14929920 | tf_op jit(solution)/shard_map/pallas_call | solution.py:42
  34.1 6.6 %collective-permute-done.4.refs_3_ = bf16[96,1152]{1,0:T(8,128)(2,1)S(1)} collective-permute-done((bf16[96,1152]{1,0:T(8,128)(2,1)S(1)}, bf16[96,1152]{1,0:T(8,128)(2,1)S(1)}, u32[]{:S(2)}, u32[]{:S(2)}) %collective-permute-start.4) | collective-permute-done | bytes 221216 | tf_op jit(solution)/shard_map/ppermute | solution.py:311
  40.7 3.8 %shard_map.78 = (bf16[512,1152]{1,0:T(8,128)(2,1)S(1)}, bf16[320,1152]{1,0:T(8,128)(2,1)S(1)}, f32[432,512]{1,0:T(8,128)S(1)}, f32[432,512]{1,0:T(8,128)S(1)}, b...) custom-call(bf16[96,1152]{1,0:T(8,128)(2,1)S(1)} %pad_maximum_fusion, ...), custom_call_target="tpu_custom_call" | custom-call | flops 1528823808 | bytes 10211328 | tf_op jit(solution)/shard_map/pallas_call | solution.py:42
  44.6 3.2 %collective-permute-start.7 = (bf16[128,1152]{1,0:T(8,128)(2,1)S(1)}, bf16[128,1152]{1,0:T(8,128)(2,1)S(1)}, u32[]{:S(2)}, u32[]{:S(2)}) collective-permute-start(bf16[128,1152]{1,0:T(8,128)(2,1)S(1)} %get-tuple-element.37), channel_id=1, source_target_pairs={{0,7},{1,0},{2,1},{3,2},{4,3},{5,4},{6,5},{7,6},{8,15},{9,8},{10,9... | collective-permute-start | bytes 884744 | tf_op jit(solution)/shard_map/ppermute | solution.py:296
  48.5 9.6 %collective-permute-done.9 = bf16[64,1152]{1,0:T(8,128)(2,1)S(1)} collective-permute-done((bf16[64,1152]{1,0:T(8,128)(2,1)S(1)}, bf16[64,1152]{1,0:T(8,128)(2,1)S(1)}, u32[]{:S(2)}, u32[]{:S(2)}) %collective-permute-start.9) | collective-permute-done | bytes 147488 | tf_op jit(solution)/shard_map/ppermute | solution.py:311
  58.3 2.8 %collective-permute-start.11 = (bf16[64,1152]{1,0:T(8,128)(2,1)S(1)}, bf16[64,1152]{1,0:T(8,128)(2,1)S(1)}, u32[]{:S(2)}, u32[]{:S(2)}) collective-permute-start(bf16[64,1152]{1,0:T(8,128)(2,1)S(1)} %get-tuple-element.68), channel_id=1, source_target_pairs={{0,2},{1,3},{2,4},{3,5},{4,6},{5,7},{6,0},{7,1},{8,10},{9,11},{10,... | collective-permute-start | bytes 442376 | tf_op jit(solution)/shard_map/ppermute | solution.py:311
  61.1 1.4 collective-permute-start.10
  62.5 1.6 collective-permute-start.13
  64.1 2.9 %collective-permute-done.11 = bf16[64,1152]{1,0:T(8,128)(2,1)S(1)} collective-permute-done((bf16[64,1152]{1,0:T(8,128)(2,1)S(1)}, bf16[64,1152]{1,0:T(8,128)(2,1)S(1)}, u32[]{:S(2)}, u32[]{:S(2)}) %collective-permute-start.11) | collective-permute-done | bytes 147488 | tf_op jit(solution)/shard_map/ppermute | solution.py:311
  66.9 0.8 collective-permute-done.10
  67.8 1.7 collective-permute-start.12
  69.5 15.1 %collective-permute-done.12 = bf16[64,1152]{1,0:T(8,128)(2,1)S(1)} collective-permute-done((bf16[64,1152]{1,0:T(8,128)(2,1)S(1)}, bf16[64,1152]{1,0:T(8,128)(2,1)S(1)}, u32[]{:S(2)}, u32[]{:S(2)}) %collective-permute-start.12) | collective-permute-done | bytes 147488 | tf_op jit(solution)/shard_map/ppermute | solution.py:299
  85.6 1.8 collective-permute-start.14
  87.4 2.6 %collective-permute-start.15 = (bf16[64,1152]{1,0:T(8,128)(2,1)S(1)}, bf16[64,1152]{1,0:T(8,128)(2,1)S(1)}, u32[]{:S(2)}, u32[]{:S(2)}) collective-permute-start(bf16[64,1152]{1,0:T(8,128)(2,1)S(1)} %fusion.2.refs_0_), channel_id=1, source_target_pairs={{0,6},{1,7},{2,0},{3,1},{4,2},{5,3},{6,4},{7,5},{8,14},{9,15},{10,... | collective-permute-start | bytes 442376 | tf_op jit(solution)/shard_map/ppermute | solution.py:311
  90.0 5.5 %collective-permute-done.14.refs_1_ = bf16[64,1152]{1,0:T(8,128)(2,1)S(1)} collective-permute-done((bf16[64,1152]{1,0:T(8,128)(2,1)S(1)}, bf16[64,1152]{1,0:T(8,128)(2,1)S(1)}, u32[]{:S(2)}, u32[]{:S(2)}) %collective-permute-start.14) | collective-permute-done | bytes 147488 | tf_op jit(solution)/shard_map/ppermute | solution.py:311
  95.5 2.1 collective-permute-start.17
  97.6 1.2 collective-permute-start.18
  98.8 1.1 collective-permute-start.16
  99.9 7.2 %collective-permute-done.16.refs_3_ = bf16[64,1152]{1,0:T(8,128)(2,1)S(1)} collective-permute-done((bf16[64,1152]{1,0:T(8,128)(2,1)S(1)}, bf16[64,1152]{1,0:T(8,128)(2,1)S(1)}, u32[]{:S(2)}, u32[]{:S(2)}) %collective-permute-start.16) | collective-permute-done | bytes 147488 | tf_op jit(solution)/shard_map/ppermute | solution.py:311
  107.5 1.0 collective-permute-done.18.refs_5_
  108.5 4.7 %shard_map.79.refs_2_ = bf16[3,432,1152]{2,1,0:T(8,128)(2,1)S(1)} custom-call(bf16[64,1152]{1,0:T(8,128)(2,1)S(1)} %fusion.2.refs_0_, bf16[64,1152]{1,0:T(8,128)(2,1)S(1)} %collective-permute-done.14.refs_1_, bf16[64,1152]{1,0:T(8,128)(2,1)S(1)} %collective-permute-done.15.refs_2_, bf16[64,1152]{1,0:T(8,128)(2,1)S(1)} %collective-permute-done.16.refs_3_, ...), custom_call_target="tpu_custom_call" | custom-call | flops 2038431744 | bytes 10543104 | tf_op jit(solution)/shard_map/pallas_call | solution.py:42
  113.2 1.0 collective-permute-start.19
  114.1 1.2 slice.71
  115.5 5.3 %shard_map.77.refs_1_ = f32[3,432,1152]{2,1,0:T(8,128)S(1)} custom-call(f32[3,432,1152]{2,1,0:T(8,128)} %get-tuple-element.33.mine, f32[3,432,1152]{2,1,0:T(8,128)} %collective-permute-done.near), custom_call_target="tpu_custom_call" | custom-call | bytes 17915904 | tf_op jit(solution)/shard_map/pallas_call | solution.py:42
  120.8 7.2 %shard_map.80 = (f32[3,432,1152]{2,1,0:T(8,128)S(1)}, f32[432,512]{1,0:T(8,128)S(1)}, f32[432,512]{1,0:T(8,128)S(1)}, bf16[432,512]{1,0:T(8,128)(2,1)S(1)}, bf16...) custom-call(s32[1]{0:T(128)} %bitcast.refs_0_.core, ...), custom_call_target="tpu_custom_call" | custom-call | flops 1528823808 | bytes 25030660 | tf_op jit(solution)/shard_map/pallas_call | solution.py:42
  128.0 1.3 collective-permute-start.21
  129.3 2.0 collective-permute-start.20
  131.3 2.2 collective-permute-start.22
  133.5 9.4 %collective-permute-done.22 = bf16[64,1152]{1,0:T(8,128)(2,1)S(1)} collective-permute-done((bf16[64,1152]{1,0:T(8,128)(2,1)S(1)}, bf16[64,1152]{1,0:T(8,128)(2,1)S(1)}, u32[]{:S(2)}, u32[]{:S(2)}) %collective-permute-start.22) | collective-permute-done | bytes 147488 | tf_op jit(solution)/shard_map/ppermute | solution.py:311
  143.0 1.9 collective-permute-start.24
  144.9 2.3 collective-permute-start.23
  147.2 3.2 %collective-permute-start.33 = (bf16[336,1152]{1,0:T(8,128)(2,1)S(1)}, bf16[336,1152]{1,0:T(8,128)(2,1)S(1)}, u32[]{:S(2)}, u32[]{:S(2)}) collective-permute-start(bf16[336,1152]{1,0:T(8,128)(2,1)S(1)} %get-tuple-element.52), channel_id=1, source_target_pairs={{0,32},{16,48},{32,0},{48,16},{64,96},{80,112},{96,64},{112,80},{1... | collective-permute-start | bytes 2322440 | tf_op jit(solution)/shard_map/ppermute | solution.py:302
  150.7 3.3 %collective-permute-done.24 = bf16[64,1152]{1,0:T(8,128)(2,1)S(1)} collective-permute-done((bf16[64,1152]{1,0:T(8,128)(2,1)S(1)}, bf16[64,1152]{1,0:T(8,128)(2,1)S(1)}, u32[]{:S(2)}, u32[]{:S(2)}) %collective-permute-start.24) | collective-permute-done | bytes 147488 | tf_op jit(solution)/shard_map/ppermute | solution.py:311
  154.1 1.9 collective-permute-start.25
  156.0 28.3 %collective-permute-done.25 = bf16[64,1152]{1,0:T(8,128)(2,1)S(1)} collective-permute-done((bf16[64,1152]{1,0:T(8,128)(2,1)S(1)}, bf16[64,1152]{1,0:T(8,128)(2,1)S(1)}, u32[]{:S(2)}, u32[]{:S(2)}) %collective-permute-start.25) | collective-permute-done | bytes 147488 | tf_op jit(solution)/shard_map/ppermute | solution.py:299
  185.0 2.1 collective-permute-start.26
  187.1 2.1 collective-permute-start.36
  189.2 1.6 collective-permute-start.32
  190.9 1.9 collective-permute-start.37
  192.8 2.7 %collective-permute-start.27 = (bf16[64,1152]{1,0:T(8,128)(2,1)S(1)}, bf16[64,1152]{1,0:T(8,128)(2,1)S(1)}, u32[]{:S(2)}, u32[]{:S(2)}) collective-permute-start(bf16[64,1152]{1,0:T(8,128)(2,1)S(1)} %collective-permute-done.26.refs_0_), channel_id=1, source_target_pairs={{0,2},{1,3},{2,4},{3,5},{4,6},{5,7},{6,0},{7,1},{8,10},{9,11},{10,... | collective-permute-start | bytes 442376 | tf_op jit(solution)/shard_map/ppermute | solution.py:311
  195.6 4.0 %collective-permute-done.37.refs_2_ = bf16[64,1152]{1,0:T(8,128)(2,1)S(1)} collective-permute-done((bf16[64,1152]{1,0:T(8,128)(2,1)S(1)}, bf16[64,1152]{1,0:T(8,128)(2,1)S(1)}, u32[]{:S(2)}, u32[]{:S(2)}) %collective-permute-start.37) | collective-permute-done | bytes 147488 | tf_op jit(solution)/shard_map/ppermute | solution.py:311
  199.6 3.6 %collective-permute-start.39 = (bf16[128,1152]{1,0:T(8,128)(2,1)S(1)}, bf16[128,1152]{1,0:T(8,128)(2,1)S(1)}, u32[]{:S(2)}, u32[]{:S(2)}) collective-permute-start(bf16[128,1152]{1,0:T(8,128)(2,1)S(1)} %constant_dynamic-update-slice_fusion.6), channel_id=1, source_target_pairs={{0,1},{1,2},{2,3},{3,4},{4,5},{5,6},{6,7},{7,0},{8,9},{9,10},{10,1... | collective-permute-start | bytes 884744 | tf_op jit(solution)/shard_map/ppermute | solution.py:296
  204.1 2.3 collective-permute-start.28
  206.4 7.5 %collective-permute-done.28.refs_2_ = bf16[64,1152]{1,0:T(8,128)(2,1)S(1)} collective-permute-done((bf16[64,1152]{1,0:T(8,128)(2,1)S(1)}, bf16[64,1152]{1,0:T(8,128)(2,1)S(1)}, u32[]{:S(2)}, u32[]{:S(2)}) %collective-permute-start.28) | collective-permute-done | bytes 147488 | tf_op jit(solution)/shard_map/ppermute | solution.py:311
  214.0 1.4 collective-permute-start.38
  215.4 8.0 %collective-permute-done.38.refs_3_ = bf16[64,1152]{1,0:T(8,128)(2,1)S(1)} collective-permute-done((bf16[64,1152]{1,0:T(8,128)(2,1)S(1)}, bf16[64,1152]{1,0:T(8,128)(2,1)S(1)}, u32[]{:S(2)}, u32[]{:S(2)}) %collective-permute-start.38) | collective-permute-done | bytes 147488 | tf_op jit(solution)/shard_map/ppermute | solution.py:311
  223.4 3.2 %collective-permute-start.31 = (bf16[128,1152]{1,0:T(8,128)(2,1)S(1)}, bf16[128,1152]{1,0:T(8,128)(2,1)S(1)}, u32[]{:S(2)}, u32[]{:S(2)}) collective-permute-start(bf16[128,1152]{1,0:T(8,128)(2,1)S(1)} %constant_dynamic-update-slice_fusion.4), channel_id=1, source_target_pairs={{0,7},{1,0},{2,1},{3,2},{4,3},{5,4},{6,5},{7,6},{8,15},{9,8},{10,9... | collective-permute-start | bytes 884744 | tf_op jit(solution)/shard_map/ppermute | solution.py:296
  226.7 4.7 %shard_map.83.refs_11_ = f32[3,432,1152]{2,1,0:T(8,128)S(1)} custom-call(bf16[64,1152]{1,0:T(8,128)(2,1)S(1)} %fusion.5.refs_0_, bf16[64,1152]{1,0:T(8,128)(2,1)S(1)} %collective-permute-done.36.refs_1_, bf16[64,1152]{1,0:T(8,128)(2,1)S(1)} %collective-permute-done.37.refs_2_, bf16[64,1152]{1,0:T(8,128)(2,1)S(1)} %collective-permute-done.38.refs_3_, ...), custom_call_target="tpu_custom_call" | custom-call | flops 2038431744 | bytes 17510400 | tf_op jit(solution)/shard_map/pallas_call | solution.py:42
  231.4 2.5 %shard_map.82 = (bf16[3,432,1152]{2,1,0:T(8,128)(2,1)S(1)}, f32[432,512]{1,0:T(8,128)S(1)}, f32[432,512]{1,0:T(8,128)S(1)}, bf16[432,512]{1,0:T(8,128)(2,1)S(1)}) custom-call(s32[1]{0:T(128)} %bitcast.refs_0_.core, bf16[512,1152]{1,0:T(8,128)(2,1)S(1)} %collective-permute-done.32.x.refs_6_, bf16[672,1152]{1,0:T(8,128)(2,1)S(1)} %shard_map.81.direct, ...), custom_call_target="tpu_custom_call" | custom-call | flops 1019215872 | bytes 9474052 | tf_op jit(solution)/shard_map/pallas_call | solution.py:42
  233.8 1.6 collective-permute-done.29.refs_3_
  235.5 4.7 %shard_map.84 = (f32[1,432,1152]{2,1,0:T(8,128)}, f32[1,432,1152]{2,1,0:T(8,128)}, f32[1,432,1152]{2,1,0:T(8,128)}) custom-call(bf16[64,1152]{1,0:T(8,128)(2,1)S(1)} %collective-permute-done.26.refs_0_, bf16[64,1152]{1,0:T(8,128)(2,1)S(1)} %collective-permute-done.27.refs_1_, bf16[64,1152]{1,0:T(8,128)(2,1)S(1)} %collective-permute-done.28.refs_2_, ...), custom_call_target="tpu_custom_call" | custom-call | flops 2038431744 | bytes 19501056 | tf_op jit(solution)/shard_map/pallas_call | solution.py:42
  (63 shorter events, 4.9 us)
Async XLA Ops:
  1.6 4.4 %collective-permute-start.1 = (bf16[32,1152]{1,0:T(8,128)(2,1)S(1)}, bf16[32,1152]{1,0:T(8,128)(2,1)S(1)}, u32[]{:S(2)}, u32[]{:S(2)}) collective-permute-start(bf16[32,1152]{1,0:T(8,128)(2,1)S(1)} %get-tuple-element.75), channel_id=1, source_target_pairs={{0,8},{1,9},{2,10},{3,11},{4,12},{5,13},{6,14},{7,15},{8,0},{9,1},... | collective-permute-start | bytes 221192 | tf_op jit(solution)/shard_map/ppermute | solution.py:299
  6.0 12.5 %collective-permute-start.2 = (bf16[96,1152]{1,0:T(8,128)(2,1)S(1)}, bf16[96,1152]{1,0:T(8,128)(2,1)S(1)}, u32[]{:S(2)}, u32[]{:S(2)}) collective-permute-start(bf16[96,1152]{1,0:T(8,128)(2,1)S(1)} %pad_maximum_fusion.1.refs_0_), channel_id=1, source_target_pairs={{0,2},{1,3},{2,4},{3,5},{4,6},{5,7},{6,0},{7,1},{8,10},{9,11},{10,... | collective-permute-start | bytes 663560 | tf_op jit(solution)/shard_map/ppermute | solution.py:311
  9.4 11.3 %collective-permute-start.3 = (bf16[96,1152]{1,0:T(8,128)(2,1)S(1)}, bf16[96,1152]{1,0:T(8,128)(2,1)S(1)}, u32[]{:S(2)}, u32[]{:S(2)}) collective-permute-start(bf16[96,1152]{1,0:T(8,128)(2,1)S(1)} %pad_maximum_fusion.1.refs_0_), channel_id=1, source_target_pairs={{0,6},{1,7},{2,0},{3,1},{4,2},{5,3},{6,4},{7,5},{8,14},{9,15},{10,... | collective-permute-start | bytes 663560 | tf_op jit(solution)/shard_map/ppermute | solution.py:311
  20.7 20.0 %collective-permute-start.5 = (bf16[192,1152]{1,0:T(8,128)(2,1)S(1)}, bf16[192,1152]{1,0:T(8,128)(2,1)S(1)}, u32[]{:S(2)}, u32[]{:S(2)}) collective-permute-start(bf16[192,1152]{1,0:T(8,128)(2,1)S(1)} %constant_dynamic-update-slice_fusion), channel_id=1, source_target_pairs={{0,1},{1,2},{2,3},{3,4},{4,5},{5,6},{6,7},{7,0},{8,9},{9,10},{10,1... | collective-permute-start | bytes 1327112 | tf_op jit(solution)/shard_map/ppermute | solution.py:296
  23.9 16.8 %collective-permute-start.6 = (bf16[192,1152]{1,0:T(8,128)(2,1)S(1)}, bf16[192,1152]{1,0:T(8,128)(2,1)S(1)}, u32[]{:S(2)}, u32[]{:S(2)}) collective-permute-start(bf16[192,1152]{1,0:T(8,128)(2,1)S(1)} %constant_dynamic-update-slice_fusion), channel_id=1, source_target_pairs={{0,7},{1,0},{2,1},{3,2},{4,3},{5,4},{6,5},{7,6},{8,15},{9,8},{10,9... | collective-permute-start | bytes 1327112 | tf_op jit(solution)/shard_map/ppermute | solution.py:296
  25.0 15.7 %collective-permute-start.4 = (bf16[96,1152]{1,0:T(8,128)(2,1)S(1)}, bf16[96,1152]{1,0:T(8,128)(2,1)S(1)}, u32[]{:S(2)}, u32[]{:S(2)}) collective-permute-start(bf16[96,1152]{1,0:T(8,128)(2,1)S(1)} %collective-permute-done.2.refs_1_), channel_id=1, source_target_pairs={{0,2},{1,3},{2,4},{3,5},{4,6},{5,7},{6,0},{7,1},{8,10},{9,11},{10,... | collective-permute-start | bytes 663560 | tf_op jit(solution)/shard_map/ppermute | solution.py:311
  26.2 1.6 copy-start
  27.8 1.6 copy-start.1
  29.3 1.6 copy-start.2
  30.9 9.8 %copy-start.4 = (bf16[2,32,1152]{2,1,0:T(8,128)(2,1)S(1)}, bf16[2,32,1152]{2,1,0:T(8,128)(2,1)}, u32[]{:S(2)}) copy-start(bf16[2,32,1152]{2,1,0:T(8,128)(2,1)} %refs_6_.1) | copy-start | bytes 442372
  44.5 40.1 %copy-start.3 = (bf16[320,1152]{1,0:T(8,128)(2,1)}, bf16[320,1152]{1,0:T(8,128)(2,1)S(1)}, u32[]{:S(2)}) copy-start(bf16[320,1152]{1,0:T(8,128)(2,1)S(1)} %get-tuple-element.41) | copy-start | bytes 2211844
  44.5 13.6 %collective-permute-start.8 = (bf16[128,1152]{1,0:T(8,128)(2,1)S(1)}, bf16[128,1152]{1,0:T(8,128)(2,1)S(1)}, u32[]{:S(2)}, u32[]{:S(2)}) collective-permute-start(bf16[128,1152]{1,0:T(8,128)(2,1)S(1)} %get-tuple-element.38), channel_id=1, source_target_pairs={{0,1},{1,2},{2,3},{3,4},{4,5},{5,6},{6,7},{7,0},{8,9},{9,10},{10,1... | collective-permute-start | bytes 884744 | tf_op jit(solution)/shard_map/ppermute | solution.py:296
  44.6 13.5 %collective-permute-start.7 = (bf16[128,1152]{1,0:T(8,128)(2,1)S(1)}, bf16[128,1152]{1,0:T(8,128)(2,1)S(1)}, u32[]{:S(2)}, u32[]{:S(2)}) collective-permute-start(bf16[128,1152]{1,0:T(8,128)(2,1)S(1)} %get-tuple-element.37), channel_id=1, source_target_pairs={{0,7},{1,0},{2,1},{3,2},{4,3},{5,4},{6,5},{7,6},{8,15},{9,8},{10,9... | collective-permute-start | bytes 884744 | tf_op jit(solution)/shard_map/ppermute | solution.py:296
  47.8 10.3 %collective-permute-start.9 = (bf16[64,1152]{1,0:T(8,128)(2,1)S(1)}, bf16[64,1152]{1,0:T(8,128)(2,1)S(1)}, u32[]{:S(2)}, u32[]{:S(2)}) collective-permute-start(bf16[64,1152]{1,0:T(8,128)(2,1)S(1)} %get-tuple-element.39), channel_id=1, source_target_pairs={{0,6},{1,7},{2,0},{3,1},{4,2},{5,3},{6,4},{7,5},{8,14},{9,15},{10,... | collective-permute-start | bytes 442376 | tf_op jit(solution)/shard_map/ppermute | solution.py:311
  58.3 8.7 %collective-permute-start.11 = (bf16[64,1152]{1,0:T(8,128)(2,1)S(1)}, bf16[64,1152]{1,0:T(8,128)(2,1)S(1)}, u32[]{:S(2)}, u32[]{:S(2)}) collective-permute-start(bf16[64,1152]{1,0:T(8,128)(2,1)S(1)} %get-tuple-element.68), channel_id=1, source_target_pairs={{0,2},{1,3},{2,4},{3,5},{4,6},{5,7},{6,0},{7,1},{8,10},{9,11},{10,... | collective-permute-start | bytes 442376 | tf_op jit(solution)/shard_map/ppermute | solution.py:311
  61.1 6.7 %collective-permute-start.10 = (bf16[64,1152]{1,0:T(8,128)(2,1)S(1)}, bf16[64,1152]{1,0:T(8,128)(2,1)S(1)}, u32[]{:S(2)}, u32[]{:S(2)}) collective-permute-start(bf16[64,1152]{1,0:T(8,128)(2,1)S(1)} %get-tuple-element.67), channel_id=1, source_target_pairs={{0,6},{1,7},{2,0},{3,1},{4,2},{5,3},{6,4},{7,5},{8,14},{9,15},{10,... | collective-permute-start | bytes 442376 | tf_op jit(solution)/shard_map/ppermute | solution.py:311
  62.5 53.0 %collective-permute-start = (f32[3,432,1152]{2,1,0:T(8,128)}, f32[3,432,1152]{2,1,0:T(8,128)}, u32[]{:S(2)}, u32[]{:S(2)}) collective-permute-start(f32[3,432,1152]{2,1,0:T(8,128)} %get-tuple-element.33.mine), channel_id=1, source_target_pairs={{0,16},{16,0},{32,48},{48,32},{64,80},{80,64},{96,112},{112,96},{1... | collective-permute-start | bytes 17915912 | tf_op jit(solution)/shard_map/ppermute | solution.py:302
  62.5 22.1 %collective-permute-start.13 = (bf16[320,1152]{1,0:T(8,128)(2,1)S(1)}, bf16[320,1152]{1,0:T(8,128)(2,1)S(1)}, u32[]{:S(2)}, u32[]{:S(2)}) collective-permute-start(bf16[320,1152]{1,0:T(8,128)(2,1)S(1)} %get-tuple-element.41), channel_id=1, source_target_pairs={{0,8},{1,9},{2,10},{3,11},{4,12},{5,13},{6,14},{7,15},{8,0},{9,1},... | collective-permute-start | bytes 2211848 | tf_op jit(solution)/shard_map/ppermute | solution.py:299
  67.8 16.7 %collective-permute-start.12 = (bf16[64,1152]{1,0:T(8,128)(2,1)S(1)}, bf16[64,1152]{1,0:T(8,128)(2,1)S(1)}, u32[]{:S(2)}, u32[]{:S(2)}) collective-permute-start(bf16[64,1152]{1,0:T(8,128)(2,1)S(1)} %fusion.6), channel_id=1, source_target_pairs={{0,8},{1,9},{2,10},{3,11},{4,12},{5,13},{6,14},{7,15},{8,0},{9,1},... | collective-permute-start | bytes 442376 | tf_op jit(solution)/shard_map/ppermute | solution.py:299
  84.6 0.9 copy-start.5
  85.6 9.9 %collective-permute-start.14 = (bf16[64,1152]{1,0:T(8,128)(2,1)S(1)}, bf16[64,1152]{1,0:T(8,128)(2,1)S(1)}, u32[]{:S(2)}, u32[]{:S(2)}) collective-permute-start(bf16[64,1152]{1,0:T(8,128)(2,1)S(1)} %fusion.2.refs_0_), channel_id=1, source_target_pairs={{0,2},{1,3},{2,4},{3,5},{4,6},{5,7},{6,0},{7,1},{8,10},{9,11},{10,... | collective-permute-start | bytes 442376 | tf_op jit(solution)/shard_map/ppermute | solution.py:311
  87.4 8.1 %collective-permute-start.15 = (bf16[64,1152]{1,0:T(8,128)(2,1)S(1)}, bf16[64,1152]{1,0:T(8,128)(2,1)S(1)}, u32[]{:S(2)}, u32[]{:S(2)}) collective-permute-start(bf16[64,1152]{1,0:T(8,128)(2,1)S(1)} %fusion.2.refs_0_), channel_id=1, source_target_pairs={{0,6},{1,7},{2,0},{3,1},{4,2},{5,3},{6,4},{7,5},{8,14},{9,15},{10,... | collective-permute-start | bytes 442376 | tf_op jit(solution)/shard_map/ppermute | solution.py:311
  95.5 12.0 %collective-permute-start.17 = (bf16[128,1152]{1,0:T(8,128)(2,1)S(1)}, bf16[128,1152]{1,0:T(8,128)(2,1)S(1)}, u32[]{:S(2)}, u32[]{:S(2)}) collective-permute-start(bf16[128,1152]{1,0:T(8,128)(2,1)S(1)} %constant_dynamic-update-slice_fusion.2), channel_id=1, source_target_pairs={{0,1},{1,2},{2,3},{3,4},{4,5},{5,6},{6,7},{7,0},{8,9},{9,10},{10,1... | collective-permute-start | bytes 884744 | tf_op jit(solution)/shard_map/ppermute | solution.py:296
  97.6 10.8 %collective-permute-start.18 = (bf16[128,1152]{1,0:T(8,128)(2,1)S(1)}, bf16[128,1152]{1,0:T(8,128)(2,1)S(1)}, u32[]{:S(2)}, u32[]{:S(2)}) collective-permute-start(bf16[128,1152]{1,0:T(8,128)(2,1)S(1)} %constant_dynamic-update-slice_fusion.2), channel_id=1, source_target_pairs={{0,7},{1,0},{2,1},{3,2},{4,3},{5,4},{6,5},{7,6},{8,15},{9,8},{10,9... | collective-permute-start | bytes 884744 | tf_op jit(solution)/shard_map/ppermute | solution.py:296
  98.8 8.3 %collective-permute-start.16 = (bf16[64,1152]{1,0:T(8,128)(2,1)S(1)}, bf16[64,1152]{1,0:T(8,128)(2,1)S(1)}, u32[]{:S(2)}, u32[]{:S(2)}) collective-permute-start(bf16[64,1152]{1,0:T(8,128)(2,1)S(1)} %collective-permute-done.14.refs_1_), channel_id=1, source_target_pairs={{0,2},{1,3},{2,4},{3,5},{4,6},{5,7},{6,0},{7,1},{8,10},{9,11},{10,... | collective-permute-start | bytes 442376 | tf_op jit(solution)/shard_map/ppermute | solution.py:311
  113.2 7.6 %collective-permute-start.19 = (bf16[3,432,1152]{2,1,0:T(8,128)(2,1)S(1)}, bf16[3,432,1152]{2,1,0:T(8,128)(2,1)}, u32[]{:S(2)}, u32[]{:S(2)}) collective-permute-start(bf16[3,432,1152]{2,1,0:T(8,128)(2,1)S(1)} %shard_map.79.refs_2_), channel_id=1, source_target_pairs={{0,16},{16,0},{32,48},{48,32},{64,80},{80,64},{96,112},{112,96},{1... | collective-permute-start | bytes 8957960 | tf_op jit(solution)/shard_map/ppermute | solution.py:302
  114.1 1.2 slice-start
  128.0 14.9 %collective-permute-start.21 = (bf16[128,1152]{1,0:T(8,128)(2,1)S(1)}, bf16[128,1152]{1,0:T(8,128)(2,1)S(1)}, u32[]{:S(2)}, u32[]{:S(2)}) collective-permute-start(bf16[128,1152]{1,0:T(8,128)(2,1)S(1)} %get-tuple-element.49), channel_id=1, source_target_pairs={{0,1},{1,2},{2,3},{3,4},{4,5},{5,6},{6,7},{7,0},{8,9},{9,10},{10,1... | collective-permute-start | bytes 884744 | tf_op jit(solution)/shard_map/ppermute | solution.py:296
  129.3 13.6 %collective-permute-start.20 = (bf16[128,1152]{1,0:T(8,128)(2,1)S(1)}, bf16[128,1152]{1,0:T(8,128)(2,1)S(1)}, u32[]{:S(2)}, u32[]{:S(2)}) collective-permute-start(bf16[128,1152]{1,0:T(8,128)(2,1)S(1)} %get-tuple-element.48), channel_id=1, source_target_pairs={{0,7},{1,0},{2,1},{3,2},{4,3},{5,4},{6,5},{7,6},{8,15},{9,8},{10,9... | collective-permute-start | bytes 884744 | tf_op jit(solution)/shard_map/ppermute | solution.py:296
  131.3 11.5 %collective-permute-start.22 = (bf16[64,1152]{1,0:T(8,128)(2,1)S(1)}, bf16[64,1152]{1,0:T(8,128)(2,1)S(1)}, u32[]{:S(2)}, u32[]{:S(2)}) collective-permute-start(bf16[64,1152]{1,0:T(8,128)(2,1)S(1)} %get-tuple-element.50), channel_id=1, source_target_pairs={{0,6},{1,7},{2,0},{3,1},{4,2},{5,3},{6,4},{7,5},{8,14},{9,15},{10,... | collective-permute-start | bytes 442376 | tf_op jit(solution)/shard_map/ppermute | solution.py:311
  143.0 11.1 %collective-permute-start.24 = (bf16[64,1152]{1,0:T(8,128)(2,1)S(1)}, bf16[64,1152]{1,0:T(8,128)(2,1)S(1)}, u32[]{:S(2)}, u32[]{:S(2)}) collective-permute-start(bf16[64,1152]{1,0:T(8,128)(2,1)S(1)} %get-tuple-element.66), channel_id=1, source_target_pairs={{0,2},{1,3},{2,4},{3,5},{4,6},{5,7},{6,0},{7,1},{8,10},{9,11},{10,... | collective-permute-start | bytes 442376 | tf_op jit(solution)/shard_map/ppermute | solution.py:311
  144.9 9.1 %collective-permute-start.23 = (bf16[64,1152]{1,0:T(8,128)(2,1)S(1)}, bf16[64,1152]{1,0:T(8,128)(2,1)S(1)}, u32[]{:S(2)}, u32[]{:S(2)}) collective-permute-start(bf16[64,1152]{1,0:T(8,128)(2,1)S(1)} %get-tuple-element.65), channel_id=1, source_target_pairs={{0,6},{1,7},{2,0},{3,1},{4,2},{5,3},{6,4},{7,5},{8,14},{9,15},{10,... | collective-permute-start | bytes 442376 | tf_op jit(solution)/shard_map/ppermute | solution.py:311
  147.2 37.2 %collective-permute-start.33 = (bf16[336,1152]{1,0:T(8,128)(2,1)S(1)}, bf16[336,1152]{1,0:T(8,128)(2,1)S(1)}, u32[]{:S(2)}, u32[]{:S(2)}) collective-permute-start(bf16[336,1152]{1,0:T(8,128)(2,1)S(1)} %get-tuple-element.52), channel_id=1, source_target_pairs={{0,32},{16,48},{32,0},{48,16},{64,96},{80,112},{96,64},{112,80},{1... | collective-permute-start | bytes 2322440 | tf_op jit(solution)/shard_map/ppermute | solution.py:302
  150.4 34.0 %collective-permute-start.34 = (bf16[336,1152]{1,0:T(8,128)(2,1)S(1)}, bf16[336,1152]{1,0:T(8,128)(2,1)S(1)}, u32[]{:S(2)}, u32[]{:S(2)}) collective-permute-start(bf16[336,1152]{1,0:T(8,128)(2,1)S(1)} %get-tuple-element.53), channel_id=1, source_target_pairs={{0,32},{16,48},{32,0},{48,16},{64,96},{80,112},{96,64},{112,80},{1... | collective-permute-start | bytes 2322440 | tf_op jit(solution)/shard_map/ppermute | solution.py:302
  154.1 30.2 %collective-permute-start.25 = (bf16[64,1152]{1,0:T(8,128)(2,1)S(1)}, bf16[64,1152]{1,0:T(8,128)(2,1)S(1)}, u32[]{:S(2)}, u32[]{:S(2)}) collective-permute-start(bf16[64,1152]{1,0:T(8,128)(2,1)S(1)} %fusion.7), channel_id=1, source_target_pairs={{0,8},{1,9},{2,10},{3,11},{4,12},{5,13},{6,14},{7,15},{8,0},{9,1},... | collective-permute-start | bytes 442376 | tf_op jit(solution)/shard_map/ppermute | solution.py:299
  184.6 46.8 %collective-permute-start.35 = (bf16[672,1152]{1,0:T(8,128)(2,1)S(1)}, bf16[672,1152]{1,0:T(8,128)(2,1)S(1)}, u32[]{:S(2)}, u32[]{:S(2)}) collective-permute-start(bf16[672,1152]{1,0:T(8,128)(2,1)S(1)} %shard_map.81.direct), channel_id=1, source_target_pairs={{0,16},{16,0},{32,48},{48,32},{64,80},{80,64},{96,112},{112,96},{1... | collective-permute-start | bytes 4644872 | tf_op jit(solution)/shard_map/ppermute | solution.py:302
  185.0 7.8 %collective-permute-start.26 = (bf16[64,1152]{1,0:T(8,128)(2,1)S(1)}, bf16[64,1152]{1,0:T(8,128)(2,1)S(1)}, u32[]{:S(2)}, u32[]{:S(2)}) collective-permute-start(bf16[64,1152]{1,0:T(8,128)(2,1)S(1)} %fusion.5.refs_0_), channel_id=1, source_target_pairs={{0,32},{16,48},{32,0},{48,16},{64,96},{80,112},{96,64},{112,80},{1... | collective-permute-start | bytes 442376 | tf_op jit(solution)/shard_map/ppermute | solution.py:302
  187.1 8.5 %collective-permute-start.36 = (bf16[64,1152]{1,0:T(8,128)(2,1)S(1)}, bf16[64,1152]{1,0:T(8,128)(2,1)S(1)}, u32[]{:S(2)}, u32[]{:S(2)}) collective-permute-start(bf16[64,1152]{1,0:T(8,128)(2,1)S(1)} %fusion.5.refs_0_), channel_id=1, source_target_pairs={{0,2},{1,3},{2,4},{3,5},{4,6},{5,7},{6,0},{7,1},{8,10},{9,11},{10,... | collective-permute-start | bytes 442376 | tf_op jit(solution)/shard_map/ppermute | solution.py:311
  189.2 42.1 %collective-permute-start.32 = (bf16[512,1152]{1,0:T(8,128)(2,1)S(1)}, bf16[512,1152]{1,0:T(8,128)(2,1)S(1)}, u32[]{:S(2)}, u32[]{:S(2)}) collective-permute-start(bf16[512,1152]{1,0:T(8,128)(2,1)S(1)} %pad_maximum_fusion.refs_4_.refs_6_), channel_id=1, source_target_pairs={{0,32},{16,48},{32,0},{48,16},{64,96},{80,112},{96,64},{112,80},{1... | collective-permute-start | bytes 3538952 | tf_op jit(solution)/shard_map/ppermute | solution.py:302
  190.9 8.7 %collective-permute-start.37 = (bf16[64,1152]{1,0:T(8,128)(2,1)S(1)}, bf16[64,1152]{1,0:T(8,128)(2,1)S(1)}, u32[]{:S(2)}, u32[]{:S(2)}) collective-permute-start(bf16[64,1152]{1,0:T(8,128)(2,1)S(1)} %fusion.5.refs_0_), channel_id=1, source_target_pairs={{0,6},{1,7},{2,0},{3,1},{4,2},{5,3},{6,4},{7,5},{8,14},{9,15},{10,... | collective-permute-start | bytes 442376 | tf_op jit(solution)/shard_map/ppermute | solution.py:311
  192.8 11.2 %collective-permute-start.27 = (bf16[64,1152]{1,0:T(8,128)(2,1)S(1)}, bf16[64,1152]{1,0:T(8,128)(2,1)S(1)}, u32[]{:S(2)}, u32[]{:S(2)}) collective-permute-start(bf16[64,1152]{1,0:T(8,128)(2,1)S(1)} %collective-permute-done.26.refs_0_), channel_id=1, source_target_pairs={{0,2},{1,3},{2,4},{3,5},{4,6},{5,7},{6,0},{7,1},{8,10},{9,11},{10,... | collective-permute-start | bytes 442376 | tf_op jit(solution)/shard_map/ppermute | solution.py:311
  199.6 23.8 %collective-permute-start.39 = (bf16[128,1152]{1,0:T(8,128)(2,1)S(1)}, bf16[128,1152]{1,0:T(8,128)(2,1)S(1)}, u32[]{:S(2)}, u32[]{:S(2)}) collective-permute-start(bf16[128,1152]{1,0:T(8,128)(2,1)S(1)} %constant_dynamic-update-slice_fusion.6), channel_id=1, source_target_pairs={{0,1},{1,2},{2,3},{3,4},{4,5},{5,6},{6,7},{7,0},{8,9},{9,10},{10,1... | collective-permute-start | bytes 884744 | tf_op jit(solution)/shard_map/ppermute | solution.py:296
  203.2 23.5 %collective-permute-start.40 = (bf16[128,1152]{1,0:T(8,128)(2,1)S(1)}, bf16[128,1152]{1,0:T(8,128)(2,1)S(1)}, u32[]{:S(2)}, u32[]{:S(2)}) collective-permute-start(bf16[128,1152]{1,0:T(8,128)(2,1)S(1)} %constant_dynamic-update-slice_fusion.6), channel_id=1, source_target_pairs={{0,7},{1,0},{2,1},{3,2},{4,3},{5,4},{6,5},{7,6},{8,15},{9,8},{10,9... | collective-permute-start | bytes 884744 | tf_op jit(solution)/shard_map/ppermute | solution.py:296
  204.1 9.9 %collective-permute-start.28 = (bf16[64,1152]{1,0:T(8,128)(2,1)S(1)}, bf16[64,1152]{1,0:T(8,128)(2,1)S(1)}, u32[]{:S(2)}, u32[]{:S(2)}) collective-permute-start(bf16[64,1152]{1,0:T(8,128)(2,1)S(1)} %collective-permute-done.26.refs_0_), channel_id=1, source_target_pairs={{0,6},{1,7},{2,0},{3,1},{4,2},{5,3},{6,4},{7,5},{8,14},{9,15},{10,... | collective-permute-start | bytes 442376 | tf_op jit(solution)/shard_map/ppermute | solution.py:311
  214.0 9.4 %collective-permute-start.38 = (bf16[64,1152]{1,0:T(8,128)(2,1)S(1)}, bf16[64,1152]{1,0:T(8,128)(2,1)S(1)}, u32[]{:S(2)}, u32[]{:S(2)}) collective-permute-start(bf16[64,1152]{1,0:T(8,128)(2,1)S(1)} %collective-permute-done.36.refs_1_), channel_id=1, source_target_pairs={{0,2},{1,3},{2,4},{3,5},{4,6},{5,7},{6,0},{7,1},{8,10},{9,11},{10,... | collective-permute-start | bytes 442376 | tf_op jit(solution)/shard_map/ppermute | solution.py:311
  223.4 12.1 %collective-permute-start.30 = (bf16[128,1152]{1,0:T(8,128)(2,1)S(1)}, bf16[128,1152]{1,0:T(8,128)(2,1)S(1)}, u32[]{:S(2)}, u32[]{:S(2)}) collective-permute-start(bf16[128,1152]{1,0:T(8,128)(2,1)S(1)} %constant_dynamic-update-slice_fusion.4), channel_id=1, source_target_pairs={{0,1},{1,2},{2,3},{3,4},{4,5},{5,6},{6,7},{7,0},{8,9},{9,10},{10,1... | collective-permute-start | bytes 884744 | tf_op jit(solution)/shard_map/ppermute | solution.py:296
  223.4 12.1 %collective-permute-start.31 = (bf16[128,1152]{1,0:T(8,128)(2,1)S(1)}, bf16[128,1152]{1,0:T(8,128)(2,1)S(1)}, u32[]{:S(2)}, u32[]{:S(2)}) collective-permute-start(bf16[128,1152]{1,0:T(8,128)(2,1)S(1)} %constant_dynamic-update-slice_fusion.4), channel_id=1, source_target_pairs={{0,7},{1,0},{2,1},{3,2},{4,3},{5,4},{6,5},{7,6},{8,15},{9,8},{10,9... | collective-permute-start | bytes 884744 | tf_op jit(solution)/shard_map/ppermute | solution.py:296
  226.7 8.8 %collective-permute-start.29 = (bf16[64,1152]{1,0:T(8,128)(2,1)S(1)}, bf16[64,1152]{1,0:T(8,128)(2,1)S(1)}, u32[]{:S(2)}, u32[]{:S(2)}) collective-permute-start(bf16[64,1152]{1,0:T(8,128)(2,1)S(1)} %collective-permute-done.27.refs_1_), channel_id=1, source_target_pairs={{0,2},{1,3},{2,4},{3,5},{4,6},{5,7},{6,0},{7,1},{8,10},{9,11},{10,... | collective-permute-start | bytes 442376 | tf_op jit(solution)/shard_map/ppermute | solution.py:311
where the time goes:
time: 241 us; the launch traced here: 240 us
  waiting for transfers between devices  123 us (51%)
  starting transfers between devices  71.6 us (30%)
  Pallas kernels  36.2 us (15%)
  local copies, waits for them, and re-layouts  7.87 us (3%)
    ppermute x18, waiting for transfers between devices, two_along(): return lax.ppermute(value, ('rep', 'hid'), pairs)  75.3 us
    ppermute x4, waiting for transfers between devices, across_y(): return lax.ppermute(value, 'hid', [(h, h ^ n_z) for h in range(n_hid)])  46.2 us
    pallas_call x9, Pallas kernels, kernel_call(): pl.pallas_call(body, out_shape=out_shape, in_specs=[VMEM_SPEC] * len(args...  36.2 us
    ppermute x18, starting transfers between devices, two_along(): return lax.ppermute(value, ('rep', 'hid'), pairs)  35 us
    ppermute x12, starting transfers between devices, along_z(): return lax.ppermute(value, 'hid', pairs)  21.3 us
    ppermute x7, starting transfers between devices, with_replica(): return lax.ppermute(value, 'rep', [(r, r ^ mask) for r in range(n_rep)])  8.55 us
    ppermute x4, starting transfers between devices, across_y(): return lax.ppermute(value, 'hid', [(h, h ^ n_z) for h in range(n_hid)])  6.78 us
    unnamed x16, local copies, waits for them, and re-layouts  5.55 us
  transfers between devices with their start and end apart: 41, of which 21 were waited for; matrix products, arithmetic and copies ran while one was open for 1% of the time, Pallas kernels for 8%

commit v1 on v0

--- a/solution.py
+++ b/solution.py
@@ -151,40 +151,42 @@
     partial_into(hidden, halves.at[2], partials, pair, True, turned)
 
 
-def gradients(residual, x, act, slope, hidden, down, scales, saved, store, tight):
+def gradients(x, act, slope, hidden, down, scales, lefts, rights, store):
     scale_model, scale_hidden = scales
+
+    def copy(start):
+        here = pl.ds(start, PART)
+        rights[0, here, :] = x[here, :]
+
+    def copy_hidden(start):
+        here = pl.ds(start, PART)
+        lefts[2, here, :] = hidden[here, :]
+
+    each_part(x.shape[0], PART, copy)
+    each_part(hidden.shape[0], PART, copy_hidden)
 
     @pl.loop(0, x.shape[0] // TOKENS)
     def _(step):
         here = pl.ds(pl.multiple_of(step * TOKENS, TOKENS), TOKENS)
-        hidden_grad = dot_nt(down[...], residual[here, :]) * scale_hidden
-        saved[0, :, here] = (hidden_grad * slope[:, here]).astype(BF16)
-        saved[1, :, here] = (hidden_grad * act[:, here]).astype(BF16)
-
-    @pl.loop(0, x.shape[1] // COLUMNS)
-    def _(step):
-        here = pl.ds(pl.multiple_of(step * COLUMNS, COLUMNS), COLUMNS)
-        store(2, step, here, dot_nn(hidden[...], residual[:, here]) * scale_hidden)
-
-        def one(i):
-            store(i, step, here, dot_nn(saved[i], x[:, here]) * scale_model)
-
-        if tight:
-            pl.loop(0, 2)(one)
-        else:
-            one(0)
-            one(1)
+        hidden_grad = dot_nt(down[...], rights[1, here, :]) * scale_hidden
+        lefts[0, :, here] = (hidden_grad * slope[:, here]).astype(BF16)
+        lefts[1, :, here] = (hidden_grad * act[:, here]).astype(BF16)
+
+    @pl.loop(0, 3)
+    def _(i):
+        scale = jnp.where(i == 2, scale_hidden, scale_model)
+        store(i, dot_nn(lefts[i], rights[i // 2]) * scale)
 
 
 def first_backward_body(pair, scales, *refs):
     blocks = refs[:6]
-    x, act, slope, hidden, halves, grads, residual, saved = refs[6:]
-    spread(blocks, residual, pair, True)
-
-    def store(i, step, columns, value):
-        grads[i, :, columns] = value.astype(BF16)
-
-    gradients(residual, x, act, slope, hidden, halves.at[2], scales, saved, store, True)
+    x, act, slope, hidden, halves, grads, lefts, rights = refs[6:]
+    spread(blocks, rights.at[1], pair, True)
+
+    def store(i, value):
+        grads[i] = value.astype(BF16)
+
+    gradients(x, act, slope, hidden, halves.at[2], scales, lefts, rights, store)
 
 
 def update_forward_body(pair, scale_model, *refs):
@@ -253,35 +255,33 @@
 
 def own_backward_body(pair, scales, *refs):
     blocks = refs[:6]
-    x, act, slope, hidden, down, weights, total, residual, saved = refs[6:]
-    spread(blocks, residual, pair, False)
-
-    def store(i, step, columns, value):
-        total[i, :, columns] = weights[i, :, columns] * 0.5 - (LEARNING_RATE * 0.5) * value
-
-    gradients(residual, x, act, slope, hidden, down, scales, saved, store, True)
+    x, act, slope, hidden, down, weights, total, lefts, rights = refs[6:]
+    spread(blocks, rights.at[1], pair, False)
+
+    def store(i, value):
+        total[i] = weights[i] * 0.5 - (LEARNING_RATE * 0.5) * value
+
+    gradients(x, act, slope, hidden, down, scales, lefts, rights, store)
 
 
 def last_body(pair, scales, *refs):
     blocks = refs[:6]
-    x, act, slope, hidden, far, total, out_gate, out_up, out_down, residual, staged, sems, saved = refs[6:]
-    outs = (out_gate, out_up, out_down)
-    spread(blocks, residual, pair, False)
-
-    def out_copy(i, step, columns):
-        return pltpu.make_async_copy(
-            staged.at[i, :, columns], outs[i].at[0, :, columns], sems.at[i, step]
-        )
-
-    def store(i, step, columns, value):
-        mean = total[i, :, columns] + far[i, :, columns].astype(F32) * 0.5
-        staged[i, :, columns] = mean - (LEARNING_RATE * 0.5) * value
-        out_copy(i, step, columns).start()
-
-    gradients(residual, x, act, slope, hidden, far.at[2], scales, saved, store, False)
-    for i in (2, 0, 1):
-        for step in range(x.shape[1] // COLUMNS):
-            out_copy(i, step, slice(step * COLUMNS, (step + 1) * COLUMNS)).wait()
+    x, act, slope, hidden, far, total, out_gate, out_up, out_down, staged, sems, lefts, rights = refs[6:]
+    spread(blocks, rights.at[1], pair, False)
+    copies = [
+        pltpu.make_async_copy(staged.at[i], out.at[0], sems.at[i])
+        for i, out in enumerate((out_gate, out_up, out_down))
+    ]
+
+    def store(i, value):
+        mean = total[i] + far[i].astype(F32) * 0.5
+        staged[i] = mean - (LEARNING_RATE * 0.5) * value
+        for k, copy in enumerate(copies):
+            pl.when(i == k)(copy.start)
+
+    gradients(x, act, slope, hidden, far.at[2], scales, lefts, rights, store)
+    for copy in copies:
+        copy.wait()
 
 
 def local(tokens, targets, w_gate, w_up, w_down, *, n_rep, n_z, hidden_units):
@@ -350,8 +350,7 @@
     acts = [arr((units, count), F32), arr((units, count), F32), arr((units, count), BF16)]
     travel = [arr((pair, width), BF16)] * 4 + [arr((2 * pair, width), BF16)] * 2
     tokens_shape = arr((count, width), BF16)
-    grad_scratch = pltpu.VMEM((2, units, count), BF16)
-    residual_scratch = pltpu.VMEM((count, width), BF16)
+    grad_scratch = (pltpu.VMEM((3, units, count), BF16), pltpu.VMEM((2, count, width), BF16))
     turned_scratch = pltpu.VMEM((count, units), BF16)
 
     first = jnp.concatenate([tokens[0], across_y(tokens[0]), tokens[1]], axis=0)
@@ -385,7 +384,7 @@
         (*blocks, x0, act, slope, hidden, halves),
         4 * product,
         LIMIT,
-        (residual_scratch, grad_scratch),
+        grad_scratch,
     )
     near_grads = with_replica(grads, 1)
 
@@ -429,7 +428,7 @@
         (*blocks, x1, act, slope, hidden, down, weights),
         4 * product,
         LIMIT,
-        (residual_scratch, grad_scratch),
+        grad_scratch,
     )
     far, act, slope, hidden = kernel_call(
         functools.partial(far_forward_body, scale_model),
@@ -447,10 +446,9 @@
         4 * product,
         LIMIT,
         (
-            residual_scratch,
             pltpu.VMEM((3, units, width), F32),
-            pltpu.SemaphoreType.DMA((3, width // COLUMNS)),
-            grad_scratch,
+            pltpu.SemaphoreType.DMA((3,)),
+            *grad_scratch,
         ),
         None,
         [pl.BlockSpec(memory_space=pl.ANY)] * 3,

time: 241 us -> 241 us (level)
  no operation moved by 1% of the time
where the time goes in v1:
time: 241 us; the launch traced here: 239 us
  waiting for transfers between devices  123 us (51%)
  starting transfers between devices  71.5 us (30%)
  Pallas kernels  34.7 us (14%)
  local copies, waits for them, and re-layouts  7.87 us (3%)
    ppermute x18, waiting for transfers between devices, two_along(): return lax.ppermute(value, ('rep', 'hid'), pairs)  75.5 us
    ppermute x4, waiting for transfers between devices, across_y(): return lax.ppermute(value, 'hid', [(h, h ^ n_z) for h in range(n_hid)])  46.2 us
    ppermute x18, starting transfers between devices, two_along(): return lax.ppermute(value, ('rep', 'hid'), pairs)  35.3 us
    pallas_call x9, Pallas kernels, kernel_call(): pl.pallas_call(body, out_shape=out_shape, in_specs=[VMEM_SPEC] * len(args...  34.7 us
    ppermute x12, starting transfers between devices, along_z(): return lax.ppermute(value, 'hid', pairs)  21 us
    ppermute x7, starting transfers between devices, with_replica(): return lax.ppermute(value, 'rep', [(r, r ^ mask) for r in range(n_rep)])  8.54 us
    ppermute x4, starting transfers between devices, across_y(): return lax.ppermute(value, 'hid', [(h, h ^ n_z) for h in range(n_hid)])  6.72 us
    unnamed x16, local copies, waits for them, and re-layouts  5.55 us
  transfers between devices with their start and end apart: 41, of which 21 were waited for; matrix products, arithmetic and copies ran while one was open for 1% of the time, Pallas kernels for 8%

profile of v1, /device:TPU:2, one launch (start us, length us, event | category | flops | bytes accessed | tf_op | source)
XLA Modules:
  0.0 239.1 jit_solution(15915230368037191224)
XLA Ops:
  0.6 0.9 slice_bitcast_fusion.3
  1.6 1.7 collective-permute-start.1
  3.2 2.8 %collective-permute-done.1 = bf16[32,1152]{1,0:T(8,128)(2,1)S(1)} collective-permute-done((bf16[32,1152]{1,0:T(8,128)(2,1)S(1)}, bf16[32,1152]{1,0:T(8,128)(2,1)S(1)}, u32[]{:S(2)}, u32[]{:S(2)}) %collective-permute-start.1) | collective-permute-done | bytes 73760 | tf_op jit(solution)/shard_map/ppermute | solution.py:299
  6.0 3.3 %collective-permute-start.2 = (bf16[96,1152]{1,0:T(8,128)(2,1)S(1)}, bf16[96,1152]{1,0:T(8,128)(2,1)S(1)}, u32[]{:S(2)}, u32[]{:S(2)}) collective-permute-start(bf16[96,1152]{1,0:T(8,128)(2,1)S(1)} %pad_maximum_fusion.1.refs_0_), channel_id=1, source_target_pairs={{0,2},{1,3},{2,4},{3,5},{4,6},{5,7},{6,0},{7,1},{8,10},{9,11},{10,... | collective-permute-start | bytes 663560 | tf_op jit(solution)/shard_map/ppermute | solution.py:311
  9.4 3.1 %collective-permute-start.3 = (bf16[96,1152]{1,0:T(8,128)(2,1)S(1)}, bf16[96,1152]{1,0:T(8,128)(2,1)S(1)}, u32[]{:S(2)}, u32[]{:S(2)}) collective-permute-start(bf16[96,1152]{1,0:T(8,128)(2,1)S(1)} %pad_maximum_fusion.1.refs_0_), channel_id=1, source_target_pairs={{0,6},{1,7},{2,0},{3,1},{4,2},{5,3},{6,4},{7,5},{8,14},{9,15},{10,... | collective-permute-start | bytes 663560 | tf_op jit(solution)/shard_map/ppermute | solution.py:311
  12.5 6.0 %collective-permute-done.2.refs_1_ = bf16[96,1152]{1,0:T(8,128)(2,1)S(1)} collective-permute-done((bf16[96,1152]{1,0:T(8,128)(2,1)S(1)}, bf16[96,1152]{1,0:T(8,128)(2,1)S(1)}, u32[]{:S(2)}, u32[]{:S(2)}) %collective-permute-start.2) | collective-permute-done | bytes 221216 | tf_op jit(solution)/shard_map/ppermute | solution.py:311
  18.5 2.2 collective-permute-done.3.refs_2_
  20.7 3.2 %collective-permute-start.5 = (bf16[192,1152]{1,0:T(8,128)(2,1)S(1)}, bf16[192,1152]{1,0:T(8,128)(2,1)S(1)}, u32[]{:S(2)}, u32[]{:S(2)}) collective-permute-start(bf16[192,1152]{1,0:T(8,128)(2,1)S(1)} %constant_dynamic-update-slice_fusion), channel_id=1, source_target_pairs={{0,1},{1,2},{2,3},{3,4},{4,5},{5,6},{6,7},{7,0},{8,9},{9,10},{10,1... | collective-permute-start | bytes 1327112 | tf_op jit(solution)/shard_map/ppermute | solution.py:296
  23.9 1.1 collective-permute-start.6
  25.0 1.2 collective-permute-start.4
  26.2 1.6 copy-done
  27.8 1.6 copy-done.1
  29.3 1.6 copy-done.2
  30.9 3.2 %shard_map.76 = (f32[3,432,1152]{2,1,0:T(8,128)}, bf16[3,432,1152]{2,1,0:T(8,128)(2,1)S(1)}) custom-call(f32[432,1152]{1,0:T(8,128)S(1)} %bitcast.12, f32[432,1152]{1,0:T(8,128)S(1)} %bitcast.13, f32[432,1152]{1,0:T(8,128)S(1)} %bitcast.14), custom_call_target="tpu_custom_call" | custom-call | bytes 14929920 | tf_op jit(solution)/shard_map/pallas_call | solution.py:42
  34.1 6.6 %collective-permute-done.4.refs_3_ = bf16[96,1152]{1,0:T(8,128)(2,1)S(1)} collective-permute-done((bf16[96,1152]{1,0:T(8,128)(2,1)S(1)}, bf16[96,1152]{1,0:T(8,128)(2,1)S(1)}, u32[]{:S(2)}, u32[]{:S(2)}) %collective-permute-start.4) | collective-permute-done | bytes 221216 | tf_op jit(solution)/shard_map/ppermute | solution.py:311
  40.7 3.8 %shard_map.78 = (bf16[512,1152]{1,0:T(8,128)(2,1)S(1)}, bf16[320,1152]{1,0:T(8,128)(2,1)S(1)}, f32[432,512]{1,0:T(8,128)S(1)}, f32[432,512]{1,0:T(8,128)S(1)}, b...) custom-call(bf16[96,1152]{1,0:T(8,128)(2,1)S(1)} %pad_maximum_fusion, ...), custom_call_target="tpu_custom_call" | custom-call | flops 1528823808 | bytes 10211328 | tf_op jit(solution)/shard_map/pallas_call | solution.py:42
  44.6 3.2 %collective-permute-start.7 = (bf16[128,1152]{1,0:T(8,128)(2,1)S(1)}, bf16[128,1152]{1,0:T(8,128)(2,1)S(1)}, u32[]{:S(2)}, u32[]{:S(2)}) collective-permute-start(bf16[128,1152]{1,0:T(8,128)(2,1)S(1)} %get-tuple-element.37), channel_id=1, source_target_pairs={{0,7},{1,0},{2,1},{3,2},{4,3},{5,4},{6,5},{7,6},{8,15},{9,8},{10,9... | collective-permute-start | bytes 884744 | tf_op jit(solution)/shard_map/ppermute | solution.py:296
  48.5 9.6 %collective-permute-done.9 = bf16[64,1152]{1,0:T(8,128)(2,1)S(1)} collective-permute-done((bf16[64,1152]{1,0:T(8,128)(2,1)S(1)}, bf16[64,1152]{1,0:T(8,128)(2,1)S(1)}, u32[]{:S(2)}, u32[]{:S(2)}) %collective-permute-start.9) | collective-permute-done | bytes 147488 | tf_op jit(solution)/shard_map/ppermute | solution.py:311
  58.3 2.8 %collective-permute-start.11 = (bf16[64,1152]{1,0:T(8,128)(2,1)S(1)}, bf16[64,1152]{1,0:T(8,128)(2,1)S(1)}, u32[]{:S(2)}, u32[]{:S(2)}) collective-permute-start(bf16[64,1152]{1,0:T(8,128)(2,1)S(1)} %get-tuple-element.68), channel_id=1, source_target_pairs={{0,2},{1,3},{2,4},{3,5},{4,6},{5,7},{6,0},{7,1},{8,10},{9,11},{10,... | collective-permute-start | bytes 442376 | tf_op jit(solution)/shard_map/ppermute | solution.py:311
  61.1 1.4 collective-permute-start.10
  62.5 1.6 collective-permute-start.13
  64.1 2.9 %collective-permute-done.11 = bf16[64,1152]{1,0:T(8,128)(2,1)S(1)} collective-permute-done((bf16[64,1152]{1,0:T(8,128)(2,1)S(1)}, bf16[64,1152]{1,0:T(8,128)(2,1)S(1)}, u32[]{:S(2)}, u32[]{:S(2)}) %collective-permute-start.11) | collective-permute-done | bytes 147488 | tf_op jit(solution)/shard_map/ppermute | solution.py:311
  67.8 1.7 collective-permute-start.12
  69.5 15.1 %collective-permute-done.12 = bf16[64,1152]{1,0:T(8,128)(2,1)S(1)} collective-permute-done((bf16[64,1152]{1,0:T(8,128)(2,1)S(1)}, bf16[64,1152]{1,0:T(8,128)(2,1)S(1)}, u32[]{:S(2)}, u32[]{:S(2)}) %collective-permute-start.12) | collective-permute-done | bytes 147488 | tf_op jit(solution)/shard_map/ppermute | solution.py:299
  85.6 1.8 collective-permute-start.14
  87.4 2.6 %collective-permute-start.15 = (bf16[64,1152]{1,0:T(8,128)(2,1)S(1)}, bf16[64,1152]{1,0:T(8,128)(2,1)S(1)}, u32[]{:S(2)}, u32[]{:S(2)}) collective-permute-start(bf16[64,1152]{1,0:T(8,128)(2,1)S(1)} %fusion.2.refs_0_), channel_id=1, source_target_pairs={{0,6},{1,7},{2,0},{3,1},{4,2},{5,3},{6,4},{7,5},{8,14},{9,15},{10,... | collective-permute-start | bytes 442376 | tf_op jit(solution)/shard_map/ppermute | solution.py:311
  90.0 5.5 %collective-permute-done.14.refs_1_ = bf16[64,1152]{1,0:T(8,128)(2,1)S(1)} collective-permute-done((bf16[64,1152]{1,0:T(8,128)(2,1)S(1)}, bf16[64,1152]{1,0:T(8,128)(2,1)S(1)}, u32[]{:S(2)}, u32[]{:S(2)}) %collective-permute-start.14) | collective-permute-done | bytes 147488 | tf_op jit(solution)/shard_map/ppermute | solution.py:311
  95.5 2.1 collective-permute-start.17
  97.6 1.2 collective-permute-start.18
  98.8 1.1 collective-permute-start.16
  99.9 7.2 %collective-permute-done.16.refs_3_ = bf16[64,1152]{1,0:T(8,128)(2,1)S(1)} collective-permute-done((bf16[64,1152]{1,0:T(8,128)(2,1)S(1)}, bf16[64,1152]{1,0:T(8,128)(2,1)S(1)}, u32[]{:S(2)}, u32[]{:S(2)}) %collective-permute-start.16) | collective-permute-done | bytes 147488 | tf_op jit(solution)/shard_map/ppermute | solution.py:311
  107.5 1.0 collective-permute-done.18.refs_5_
  108.5 3.7 %shard_map.79.refs_2_ = bf16[3,432,1152]{2,1,0:T(8,128)(2,1)S(1)} custom-call(bf16[64,1152]{1,0:T(8,128)(2,1)S(1)} %fusion.2.refs_0_, bf16[64,1152]{1,0:T(8,128)(2,1)S(1)} %collective-permute-done.14.refs_1_, bf16[64,1152]{1,0:T(8,128)(2,1)S(1)} %collective-permute-done.15.refs_2_, bf16[64,1152]{1,0:T(8,128)(2,1)S(1)} %collective-permute-done.16.refs_3_, ...), custom_call_target="tpu_custom_call" | custom-call | flops 2038431744 | bytes 10543104 | tf_op jit(solution)/shard_map/pallas_call | solution.py:42
  112.2 1.0 collective-permute-start.19
  113.2 1.2 slice.71
  114.5 5.3 %shard_map.77.refs_1_ = f32[3,432,1152]{2,1,0:T(8,128)S(1)} custom-call(f32[3,432,1152]{2,1,0:T(8,128)} %get-tuple-element.33.mine, f32[3,432,1152]{2,1,0:T(8,128)} %collective-permute-done.near), custom_call_target="tpu_custom_call" | custom-call | bytes 17915904 | tf_op jit(solution)/shard_map/pallas_call | solution.py:42
  119.8 7.2 %shard_map.80 = (f32[3,432,1152]{2,1,0:T(8,128)S(1)}, f32[432,512]{1,0:T(8,128)S(1)}, f32[432,512]{1,0:T(8,128)S(1)}, bf16[432,512]{1,0:T(8,128)(2,1)S(1)}, bf16...) custom-call(s32[1]{0:T(128)} %bitcast.refs_0_.core, ...), custom_call_target="tpu_custom_call" | custom-call | flops 1528823808 | bytes 25030660 | tf_op jit(solution)/shard_map/pallas_call | solution.py:42
  127.0 1.3 collective-permute-start.21
  128.3 2.0 collective-permute-start.20
  130.3 2.2 collective-permute-start.22
  132.5 9.4 %collective-permute-done.22 = bf16[64,1152]{1,0:T(8,128)(2,1)S(1)} collective-permute-done((bf16[64,1152]{1,0:T(8,128)(2,1)S(1)}, bf16[64,1152]{1,0:T(8,128)(2,1)S(1)}, u32[]{:S(2)}, u32[]{:S(2)}) %collective-permute-start.22) | collective-permute-done | bytes 147488 | tf_op jit(solution)/shard_map/ppermute | solution.py:311
  142.0 1.9 collective-permute-start.24
  143.9 2.3 collective-permute-start.23
  146.2 3.2 %collective-permute-start.33 = (bf16[336,1152]{1,0:T(8,128)(2,1)S(1)}, bf16[336,1152]{1,0:T(8,128)(2,1)S(1)}, u32[]{:S(2)}, u32[]{:S(2)}) collective-permute-start(bf16[336,1152]{1,0:T(8,128)(2,1)S(1)} %get-tuple-element.52), channel_id=1, source_target_pairs={{0,32},{16,48},{32,0},{48,16},{64,96},{80,112},{96,64},{112,80},{1... | collective-permute-start | bytes 2322440 | tf_op jit(solution)/shard_map/ppermute | solution.py:302
  149.8 3.3 %collective-permute-done.24 = bf16[64,1152]{1,0:T(8,128)(2,1)S(1)} collective-permute-done((bf16[64,1152]{1,0:T(8,128)(2,1)S(1)}, bf16[64,1152]{1,0:T(8,128)(2,1)S(1)}, u32[]{:S(2)}, u32[]{:S(2)}) %collective-permute-start.24) | collective-permute-done | bytes 147488 | tf_op jit(solution)/shard_map/ppermute | solution.py:311
  153.2 1.8 collective-permute-start.25
  155.0 28.4 %collective-permute-done.25 = bf16[64,1152]{1,0:T(8,128)(2,1)S(1)} collective-permute-done((bf16[64,1152]{1,0:T(8,128)(2,1)S(1)}, bf16[64,1152]{1,0:T(8,128)(2,1)S(1)}, u32[]{:S(2)}, u32[]{:S(2)}) %collective-permute-start.25) | collective-permute-done | bytes 147488 | tf_op jit(solution)/shard_map/ppermute | solution.py:299
  184.0 2.1 collective-permute-start.26
  186.1 2.2 collective-permute-start.36
  188.3 1.7 collective-permute-start.32
  189.9 1.9 collective-permute-start.37
  191.9 2.7 %collective-permute-start.27 = (bf16[64,1152]{1,0:T(8,128)(2,1)S(1)}, bf16[64,1152]{1,0:T(8,128)(2,1)S(1)}, u32[]{:S(2)}, u32[]{:S(2)}) collective-permute-start(bf16[64,1152]{1,0:T(8,128)(2,1)S(1)} %collective-permute-done.26.refs_0_), channel_id=1, source_target_pairs={{0,2},{1,3},{2,4},{3,5},{4,6},{5,7},{6,0},{7,1},{8,10},{9,11},{10,... | collective-permute-start | bytes 442376 | tf_op jit(solution)/shard_map/ppermute | solution.py:311
  194.6 4.0 %collective-permute-done.37.refs_2_ = bf16[64,1152]{1,0:T(8,128)(2,1)S(1)} collective-permute-done((bf16[64,1152]{1,0:T(8,128)(2,1)S(1)}, bf16[64,1152]{1,0:T(8,128)(2,1)S(1)}, u32[]{:S(2)}, u32[]{:S(2)}) %collective-permute-start.37) | collective-permute-done | bytes 147488 | tf_op jit(solution)/shard_map/ppermute | solution.py:311
  198.7 3.5 %collective-permute-start.39 = (bf16[128,1152]{1,0:T(8,128)(2,1)S(1)}, bf16[128,1152]{1,0:T(8,128)(2,1)S(1)}, u32[]{:S(2)}, u32[]{:S(2)}) collective-permute-start(bf16[128,1152]{1,0:T(8,128)(2,1)S(1)} %constant_dynamic-update-slice_fusion.6), channel_id=1, source_target_pairs={{0,1},{1,2},{2,3},{3,4},{4,5},{5,6},{6,7},{7,0},{8,9},{9,10},{10,1... | collective-permute-start | bytes 884744 | tf_op jit(solution)/shard_map/ppermute | solution.py:296
  202.2 0.9 collective-permute-done.27.refs_1_
  203.1 2.3 collective-permute-start.28
  205.5 7.4 %collective-permute-done.28.refs_2_ = bf16[64,1152]{1,0:T(8,128)(2,1)S(1)} collective-permute-done((bf16[64,1152]{1,0:T(8,128)(2,1)S(1)}, bf16[64,1152]{1,0:T(8,128)(2,1)S(1)}, u32[]{:S(2)}, u32[]{:S(2)}) %collective-permute-start.28) | collective-permute-done | bytes 147488 | tf_op jit(solution)/shard_map/ppermute | solution.py:311
  212.8 1.6 collective-permute-start.38
  214.5 7.6 %collective-permute-done.38.refs_3_ = bf16[64,1152]{1,0:T(8,128)(2,1)S(1)} collective-permute-done((bf16[64,1152]{1,0:T(8,128)(2,1)S(1)}, bf16[64,1152]{1,0:T(8,128)(2,1)S(1)}, u32[]{:S(2)}, u32[]{:S(2)}) %collective-permute-start.38) | collective-permute-done | bytes 147488 | tf_op jit(solution)/shard_map/ppermute | solution.py:311
  222.1 3.2 %collective-permute-start.31 = (bf16[128,1152]{1,0:T(8,128)(2,1)S(1)}, bf16[128,1152]{1,0:T(8,128)(2,1)S(1)}, u32[]{:S(2)}, u32[]{:S(2)}) collective-permute-start(bf16[128,1152]{1,0:T(8,128)(2,1)S(1)} %constant_dynamic-update-slice_fusion.4), channel_id=1, source_target_pairs={{0,7},{1,0},{2,1},{3,2},{4,3},{5,4},{6,5},{7,6},{8,15},{9,8},{10,9... | collective-permute-start | bytes 884744 | tf_op jit(solution)/shard_map/ppermute | solution.py:296
  225.3 3.8 %shard_map.83.refs_11_ = f32[3,432,1152]{2,1,0:T(8,128)S(1)} custom-call(bf16[64,1152]{1,0:T(8,128)(2,1)S(1)} %fusion.5.refs_0_, bf16[64,1152]{1,0:T(8,128)(2,1)S(1)} %collective-permute-done.36.refs_1_, bf16[64,1152]{1,0:T(8,128)(2,1)S(1)} %collective-permute-done.37.refs_2_, bf16[64,1152]{1,0:T(8,128)(2,1)S(1)} %collective-permute-done.38.refs_3_, ...), custom_call_target="tpu_custom_call" | custom-call | flops 2038431744 | bytes 17510400 | tf_op jit(solution)/shard_map/pallas_call | solution.py:42
  229.2 2.5 %shard_map.82 = (bf16[3,432,1152]{2,1,0:T(8,128)(2,1)S(1)}, f32[432,512]{1,0:T(8,128)S(1)}, f32[432,512]{1,0:T(8,128)S(1)}, bf16[432,512]{1,0:T(8,128)(2,1)S(1)}) custom-call(s32[1]{0:T(128)} %bitcast.refs_0_.core, bf16[512,1152]{1,0:T(8,128)(2,1)S(1)} %collective-permute-done.32.x.refs_6_, bf16[672,1152]{1,0:T(8,128)(2,1)S(1)} %shard_map.81.direct, ...), custom_call_target="tpu_custom_call" | custom-call | flops 1019215872 | bytes 9474052 | tf_op jit(solution)/shard_map/pallas_call | solution.py:42
  231.6 2.1 collective-permute-done.29.refs_3_
  233.8 5.2 %shard_map.84 = (f32[1,432,1152]{2,1,0:T(8,128)}, f32[1,432,1152]{2,1,0:T(8,128)}, f32[1,432,1152]{2,1,0:T(8,128)}) custom-call(bf16[64,1152]{1,0:T(8,128)(2,1)S(1)} %collective-permute-done.26.refs_0_, bf16[64,1152]{1,0:T(8,128)(2,1)S(1)} %collective-permute-done.27.refs_1_, bf16[64,1152]{1,0:T(8,128)(2,1)S(1)} %collective-permute-done.28.refs_2_, ...), custom_call_target="tpu_custom_call" | custom-call | flops 2038431744 | bytes 19501056 | tf_op jit(solution)/shard_map/pallas_call | solution.py:42
  (63 shorter events, 4.8 us)
Async XLA Ops:
  1.6 4.4 %collective-permute-start.1 = (bf16[32,1152]{1,0:T(8,128)(2,1)S(1)}, bf16[32,1152]{1,0:T(8,128)(2,1)S(1)}, u32[]{:S(2)}, u32[]{:S(2)}) collective-permute-start(bf16[32,1152]{1,0:T(8,128)(2,1)S(1)} %get-tuple-element.75), channel_id=1, source_target_pairs={{0,8},{1,9},{2,10},{3,11},{4,12},{5,13},{6,14},{7,15},{8,0},{9,1},... | collective-permute-start | bytes 221192 | tf_op jit(solution)/shard_map/ppermute | solution.py:299
  6.0 12.5 %collective-permute-start.2 = (bf16[96,1152]{1,0:T(8,128)(2,1)S(1)}, bf16[96,1152]{1,0:T(8,128)(2,1)S(1)}, u32[]{:S(2)}, u32[]{:S(2)}) collective-permute-start(bf16[96,1152]{1,0:T(8,128)(2,1)S(1)} %pad_maximum_fusion.1.refs_0_), channel_id=1, source_target_pairs={{0,2},{1,3},{2,4},{3,5},{4,6},{5,7},{6,0},{7,1},{8,10},{9,11},{10,... | collective-permute-start | bytes 663560 | tf_op jit(solution)/shard_map/ppermute | solution.py:311
  9.4 11.3 %collective-permute-start.3 = (bf16[96,1152]{1,0:T(8,128)(2,1)S(1)}, bf16[96,1152]{1,0:T(8,128)(2,1)S(1)}, u32[]{:S(2)}, u32[]{:S(2)}) collective-permute-start(bf16[96,1152]{1,0:T(8,128)(2,1)S(1)} %pad_maximum_fusion.1.refs_0_), channel_id=1, source_target_pairs={{0,6},{1,7},{2,0},{3,1},{4,2},{5,3},{6,4},{7,5},{8,14},{9,15},{10,... | collective-permute-start | bytes 663560 | tf_op jit(solution)/shard_map/ppermute | solution.py:311
  20.7 20.0 %collective-permute-start.5 = (bf16[192,1152]{1,0:T(8,128)(2,1)S(1)}, bf16[192,1152]{1,0:T(8,128)(2,1)S(1)}, u32[]{:S(2)}, u32[]{:S(2)}) collective-permute-start(bf16[192,1152]{1,0:T(8,128)(2,1)S(1)} %constant_dynamic-update-slice_fusion), channel_id=1, source_target_pairs={{0,1},{1,2},{2,3},{3,4},{4,5},{5,6},{6,7},{7,0},{8,9},{9,10},{10,1... | collective-permute-start | bytes 1327112 | tf_op jit(solution)/shard_map/ppermute | solution.py:296
  23.9 16.8 %collective-permute-start.6 = (bf16[192,1152]{1,0:T(8,128)(2,1)S(1)}, bf16[192,1152]{1,0:T(8,128)(2,1)S(1)}, u32[]{:S(2)}, u32[]{:S(2)}) collective-permute-start(bf16[192,1152]{1,0:T(8,128)(2,1)S(1)} %constant_dynamic-update-slice_fusion), channel_id=1, source_target_pairs={{0,7},{1,0},{2,1},{3,2},{4,3},{5,4},{6,5},{7,6},{8,15},{9,8},{10,9... | collective-permute-start | bytes 1327112 | tf_op jit(solution)/shard_map/ppermute | solution.py:296
  25.0 15.7 %collective-permute-start.4 = (bf16[96,1152]{1,0:T(8,128)(2,1)S(1)}, bf16[96,1152]{1,0:T(8,128)(2,1)S(1)}, u32[]{:S(2)}, u32[]{:S(2)}) collective-permute-start(bf16[96,1152]{1,0:T(8,128)(2,1)S(1)} %collective-permute-done.2.refs_1_), channel_id=1, source_target_pairs={{0,2},{1,3},{2,4},{3,5},{4,6},{5,7},{6,0},{7,1},{8,10},{9,11},{10,... | collective-permute-start | bytes 663560 | tf_op jit(solution)/shard_map/ppermute | solution.py:311
  26.2 1.6 copy-start
  27.8 1.6 copy-start.1
  29.3 1.6 copy-start.2
  30.9 9.8 %copy-start.4 = (bf16[2,32,1152]{2,1,0:T(8,128)(2,1)S(1)}, bf16[2,32,1152]{2,1,0:T(8,128)(2,1)}, u32[]{:S(2)}) copy-start(bf16[2,32,1152]{2,1,0:T(8,128)(2,1)} %refs_6_.1) | copy-start | bytes 442372
  44.5 40.1 %copy-start.3 = (bf16[320,1152]{1,0:T(8,128)(2,1)}, bf16[320,1152]{1,0:T(8,128)(2,1)S(1)}, u32[]{:S(2)}) copy-start(bf16[320,1152]{1,0:T(8,128)(2,1)S(1)} %get-tuple-element.41) | copy-start | bytes 2211844
  44.5 13.6 %collective-permute-start.8 = (bf16[128,1152]{1,0:T(8,128)(2,1)S(1)}, bf16[128,1152]{1,0:T(8,128)(2,1)S(1)}, u32[]{:S(2)}, u32[]{:S(2)}) collective-permute-start(bf16[128,1152]{1,0:T(8,128)(2,1)S(1)} %get-tuple-element.38), channel_id=1, source_target_pairs={{0,1},{1,2},{2,3},{3,4},{4,5},{5,6},{6,7},{7,0},{8,9},{9,10},{10,1... | collective-permute-start | bytes 884744 | tf_op jit(solution)/shard_map/ppermute | solution.py:296
  44.6 13.5 %collective-permute-start.7 = (bf16[128,1152]{1,0:T(8,128)(2,1)S(1)}, bf16[128,1152]{1,0:T(8,128)(2,1)S(1)}, u32[]{:S(2)}, u32[]{:S(2)}) collective-permute-start(bf16[128,1152]{1,0:T(8,128)(2,1)S(1)} %get-tuple-element.37), channel_id=1, source_target_pairs={{0,7},{1,0},{2,1},{3,2},{4,3},{5,4},{6,5},{7,6},{8,15},{9,8},{10,9... | collective-permute-start | bytes 884744 | tf_op jit(solution)/shard_map/ppermute | solution.py:296
  47.8 10.3 %collective-permute-start.9 = (bf16[64,1152]{1,0:T(8,128)(2,1)S(1)}, bf16[64,1152]{1,0:T(8,128)(2,1)S(1)}, u32[]{:S(2)}, u32[]{:S(2)}) collective-permute-start(bf16[64,1152]{1,0:T(8,128)(2,1)S(1)} %get-tuple-element.39), channel_id=1, source_target_pairs={{0,6},{1,7},{2,0},{3,1},{4,2},{5,3},{6,4},{7,5},{8,14},{9,15},{10,... | collective-permute-start | bytes 442376 | tf_op jit(solution)/shard_map/ppermute | solution.py:311
  58.3 8.7 %collective-permute-start.11 = (bf16[64,1152]{1,0:T(8,128)(2,1)S(1)}, bf16[64,1152]{1,0:T(8,128)(2,1)S(1)}, u32[]{:S(2)}, u32[]{:S(2)}) collective-permute-start(bf16[64,1152]{1,0:T(8,128)(2,1)S(1)} %get-tuple-element.68), channel_id=1, source_target_pairs={{0,2},{1,3},{2,4},{3,5},{4,6},{5,7},{6,0},{7,1},{8,10},{9,11},{10,... | collective-permute-start | bytes 442376 | tf_op jit(solution)/shard_map/ppermute | solution.py:311
  61.1 6.7 %collective-permute-start.10 = (bf16[64,1152]{1,0:T(8,128)(2,1)S(1)}, bf16[64,1152]{1,0:T(8,128)(2,1)S(1)}, u32[]{:S(2)}, u32[]{:S(2)}) collective-permute-start(bf16[64,1152]{1,0:T(8,128)(2,1)S(1)} %get-tuple-element.67), channel_id=1, source_target_pairs={{0,6},{1,7},{2,0},{3,1},{4,2},{5,3},{6,4},{7,5},{8,14},{9,15},{10,... | collective-permute-start | bytes 442376 | tf_op jit(solution)/shard_map/ppermute | solution.py:311
  62.5 52.0 %collective-permute-start = (f32[3,432,1152]{2,1,0:T(8,128)}, f32[3,432,1152]{2,1,0:T(8,128)}, u32[]{:S(2)}, u32[]{:S(2)}) collective-permute-start(f32[3,432,1152]{2,1,0:T(8,128)} %get-tuple-element.33.mine), channel_id=1, source_target_pairs={{0,16},{16,0},{32,48},{48,32},{64,80},{80,64},{96,112},{112,96},{1... | collective-permute-start | bytes 17915912 | tf_op jit(solution)/shard_map/ppermute | solution.py:302
  62.5 22.1 %collective-permute-start.13 = (bf16[320,1152]{1,0:T(8,128)(2,1)S(1)}, bf16[320,1152]{1,0:T(8,128)(2,1)S(1)}, u32[]{:S(2)}, u32[]{:S(2)}) collective-permute-start(bf16[320,1152]{1,0:T(8,128)(2,1)S(1)} %get-tuple-element.41), channel_id=1, source_target_pairs={{0,8},{1,9},{2,10},{3,11},{4,12},{5,13},{6,14},{7,15},{8,0},{9,1},... | collective-permute-start | bytes 2211848 | tf_op jit(solution)/shard_map/ppermute | solution.py:299
  67.8 16.7 %collective-permute-start.12 = (bf16[64,1152]{1,0:T(8,128)(2,1)S(1)}, bf16[64,1152]{1,0:T(8,128)(2,1)S(1)}, u32[]{:S(2)}, u32[]{:S(2)}) collective-permute-start(bf16[64,1152]{1,0:T(8,128)(2,1)S(1)} %fusion.6), channel_id=1, source_target_pairs={{0,8},{1,9},{2,10},{3,11},{4,12},{5,13},{6,14},{7,15},{8,0},{9,1},... | collective-permute-start | bytes 442376 | tf_op jit(solution)/shard_map/ppermute | solution.py:299
  84.6 0.9 copy-start.5
  85.6 9.9 %collective-permute-start.14 = (bf16[64,1152]{1,0:T(8,128)(2,1)S(1)}, bf16[64,1152]{1,0:T(8,128)(2,1)S(1)}, u32[]{:S(2)}, u32[]{:S(2)}) collective-permute-start(bf16[64,1152]{1,0:T(8,128)(2,1)S(1)} %fusion.2.refs_0_), channel_id=1, source_target_pairs={{0,2},{1,3},{2,4},{3,5},{4,6},{5,7},{6,0},{7,1},{8,10},{9,11},{10,... | collective-permute-start | bytes 442376 | tf_op jit(solution)/shard_map/ppermute | solution.py:311
  87.4 8.1 %collective-permute-start.15 = (bf16[64,1152]{1,0:T(8,128)(2,1)S(1)}, bf16[64,1152]{1,0:T(8,128)(2,1)S(1)}, u32[]{:S(2)}, u32[]{:S(2)}) collective-permute-start(bf16[64,1152]{1,0:T(8,128)(2,1)S(1)} %fusion.2.refs_0_), channel_id=1, source_target_pairs={{0,6},{1,7},{2,0},{3,1},{4,2},{5,3},{6,4},{7,5},{8,14},{9,15},{10,... | collective-permute-start | bytes 442376 | tf_op jit(solution)/shard_map/ppermute | solution.py:311
  95.5 12.0 %collective-permute-start.17 = (bf16[128,1152]{1,0:T(8,128)(2,1)S(1)}, bf16[128,1152]{1,0:T(8,128)(2,1)S(1)}, u32[]{:S(2)}, u32[]{:S(2)}) collective-permute-start(bf16[128,1152]{1,0:T(8,128)(2,1)S(1)} %constant_dynamic-update-slice_fusion.2), channel_id=1, source_target_pairs={{0,1},{1,2},{2,3},{3,4},{4,5},{5,6},{6,7},{7,0},{8,9},{9,10},{10,1... | collective-permute-start | bytes 884744 | tf_op jit(solution)/shard_map/ppermute | solution.py:296
  97.6 10.8 %collective-permute-start.18 = (bf16[128,1152]{1,0:T(8,128)(2,1)S(1)}, bf16[128,1152]{1,0:T(8,128)(2,1)S(1)}, u32[]{:S(2)}, u32[]{:S(2)}) collective-permute-start(bf16[128,1152]{1,0:T(8,128)(2,1)S(1)} %constant_dynamic-update-slice_fusion.2), channel_id=1, source_target_pairs={{0,7},{1,0},{2,1},{3,2},{4,3},{5,4},{6,5},{7,6},{8,15},{9,8},{10,9... | collective-permute-start | bytes 884744 | tf_op jit(solution)/shard_map/ppermute | solution.py:296
  98.8 8.3 %collective-permute-start.16 = (bf16[64,1152]{1,0:T(8,128)(2,1)S(1)}, bf16[64,1152]{1,0:T(8,128)(2,1)S(1)}, u32[]{:S(2)}, u32[]{:S(2)}) collective-permute-start(bf16[64,1152]{1,0:T(8,128)(2,1)S(1)} %collective-permute-done.14.refs_1_), channel_id=1, source_target_pairs={{0,2},{1,3},{2,4},{3,5},{4,6},{5,7},{6,0},{7,1},{8,10},{9,11},{10,... | collective-permute-start | bytes 442376 | tf_op jit(solution)/shard_map/ppermute | solution.py:311
  112.2 7.6 %collective-permute-start.19 = (bf16[3,432,1152]{2,1,0:T(8,128)(2,1)S(1)}, bf16[3,432,1152]{2,1,0:T(8,128)(2,1)}, u32[]{:S(2)}, u32[]{:S(2)}) collective-permute-start(bf16[3,432,1152]{2,1,0:T(8,128)(2,1)S(1)} %shard_map.79.refs_2_), channel_id=1, source_target_pairs={{0,16},{16,0},{32,48},{48,32},{64,80},{80,64},{96,112},{112,96},{1... | collective-permute-start | bytes 8957960 | tf_op jit(solution)/shard_map/ppermute | solution.py:302
  113.2 1.2 slice-start
  127.0 14.9 %collective-permute-start.21 = (bf16[128,1152]{1,0:T(8,128)(2,1)S(1)}, bf16[128,1152]{1,0:T(8,128)(2,1)S(1)}, u32[]{:S(2)}, u32[]{:S(2)}) collective-permute-start(bf16[128,1152]{1,0:T(8,128)(2,1)S(1)} %get-tuple-element.49), channel_id=1, source_target_pairs={{0,1},{1,2},{2,3},{3,4},{4,5},{5,6},{6,7},{7,0},{8,9},{9,10},{10,1... | collective-permute-start | bytes 884744 | tf_op jit(solution)/shard_map/ppermute | solution.py:296
  128.3 13.6 %collective-permute-start.20 = (bf16[128,1152]{1,0:T(8,128)(2,1)S(1)}, bf16[128,1152]{1,0:T(8,128)(2,1)S(1)}, u32[]{:S(2)}, u32[]{:S(2)}) collective-permute-start(bf16[128,1152]{1,0:T(8,128)(2,1)S(1)} %get-tuple-element.48), channel_id=1, source_target_pairs={{0,7},{1,0},{2,1},{3,2},{4,3},{5,4},{6,5},{7,6},{8,15},{9,8},{10,9... | collective-permute-start | bytes 884744 | tf_op jit(solution)/shard_map/ppermute | solution.py:296
  130.3 11.6 %collective-permute-start.22 = (bf16[64,1152]{1,0:T(8,128)(2,1)S(1)}, bf16[64,1152]{1,0:T(8,128)(2,1)S(1)}, u32[]{:S(2)}, u32[]{:S(2)}) collective-permute-start(bf16[64,1152]{1,0:T(8,128)(2,1)S(1)} %get-tuple-element.50), channel_id=1, source_target_pairs={{0,6},{1,7},{2,0},{3,1},{4,2},{5,3},{6,4},{7,5},{8,14},{9,15},{10,... | collective-permute-start | bytes 442376 | tf_op jit(solution)/shard_map/ppermute | solution.py:311
  142.0 11.1 %collective-permute-start.24 = (bf16[64,1152]{1,0:T(8,128)(2,1)S(1)}, bf16[64,1152]{1,0:T(8,128)(2,1)S(1)}, u32[]{:S(2)}, u32[]{:S(2)}) collective-permute-start(bf16[64,1152]{1,0:T(8,128)(2,1)S(1)} %get-tuple-element.66), channel_id=1, source_target_pairs={{0,2},{1,3},{2,4},{3,5},{4,6},{5,7},{6,0},{7,1},{8,10},{9,11},{10,... | collective-permute-start | bytes 442376 | tf_op jit(solution)/shard_map/ppermute | solution.py:311
  143.9 9.2 %collective-permute-start.23 = (bf16[64,1152]{1,0:T(8,128)(2,1)S(1)}, bf16[64,1152]{1,0:T(8,128)(2,1)S(1)}, u32[]{:S(2)}, u32[]{:S(2)}) collective-permute-start(bf16[64,1152]{1,0:T(8,128)(2,1)S(1)} %get-tuple-element.65), channel_id=1, source_target_pairs={{0,6},{1,7},{2,0},{3,1},{4,2},{5,3},{6,4},{7,5},{8,14},{9,15},{10,... | collective-permute-start | bytes 442376 | tf_op jit(solution)/shard_map/ppermute | solution.py:311
  146.2 37.2 %collective-permute-start.33 = (bf16[336,1152]{1,0:T(8,128)(2,1)S(1)}, bf16[336,1152]{1,0:T(8,128)(2,1)S(1)}, u32[]{:S(2)}, u32[]{:S(2)}) collective-permute-start(bf16[336,1152]{1,0:T(8,128)(2,1)S(1)} %get-tuple-element.52), channel_id=1, source_target_pairs={{0,32},{16,48},{32,0},{48,16},{64,96},{80,112},{96,64},{112,80},{1... | collective-permute-start | bytes 2322440 | tf_op jit(solution)/shard_map/ppermute | solution.py:302
  149.4 34.0 %collective-permute-start.34 = (bf16[336,1152]{1,0:T(8,128)(2,1)S(1)}, bf16[336,1152]{1,0:T(8,128)(2,1)S(1)}, u32[]{:S(2)}, u32[]{:S(2)}) collective-permute-start(bf16[336,1152]{1,0:T(8,128)(2,1)S(1)} %get-tuple-element.53), channel_id=1, source_target_pairs={{0,32},{16,48},{32,0},{48,16},{64,96},{80,112},{96,64},{112,80},{1... | collective-permute-start | bytes 2322440 | tf_op jit(solution)/shard_map/ppermute | solution.py:302
  153.2 30.2 %collective-permute-start.25 = (bf16[64,1152]{1,0:T(8,128)(2,1)S(1)}, bf16[64,1152]{1,0:T(8,128)(2,1)S(1)}, u32[]{:S(2)}, u32[]{:S(2)}) collective-permute-start(bf16[64,1152]{1,0:T(8,128)(2,1)S(1)} %fusion.7), channel_id=1, source_target_pairs={{0,8},{1,9},{2,10},{3,11},{4,12},{5,13},{6,14},{7,15},{8,0},{9,1},... | collective-permute-start | bytes 442376 | tf_op jit(solution)/shard_map/ppermute | solution.py:299
  183.6 45.6 %collective-permute-start.35 = (bf16[672,1152]{1,0:T(8,128)(2,1)S(1)}, bf16[672,1152]{1,0:T(8,128)(2,1)S(1)}, u32[]{:S(2)}, u32[]{:S(2)}) collective-permute-start(bf16[672,1152]{1,0:T(8,128)(2,1)S(1)} %shard_map.81.direct), channel_id=1, source_target_pairs={{0,16},{16,0},{32,48},{48,32},{64,80},{80,64},{96,112},{112,96},{1... | collective-permute-start | bytes 4644872 | tf_op jit(solution)/shard_map/ppermute | solution.py:302
  184.0 7.8 %collective-permute-start.26 = (bf16[64,1152]{1,0:T(8,128)(2,1)S(1)}, bf16[64,1152]{1,0:T(8,128)(2,1)S(1)}, u32[]{:S(2)}, u32[]{:S(2)}) collective-permute-start(bf16[64,1152]{1,0:T(8,128)(2,1)S(1)} %fusion.5.refs_0_), channel_id=1, source_target_pairs={{0,32},{16,48},{32,0},{48,16},{64,96},{80,112},{96,64},{112,80},{1... | collective-permute-start | bytes 442376 | tf_op jit(solution)/shard_map/ppermute | solution.py:302
  186.1 8.5 %collective-permute-start.36 = (bf16[64,1152]{1,0:T(8,128)(2,1)S(1)}, bf16[64,1152]{1,0:T(8,128)(2,1)S(1)}, u32[]{:S(2)}, u32[]{:S(2)}) collective-permute-start(bf16[64,1152]{1,0:T(8,128)(2,1)S(1)} %fusion.5.refs_0_), channel_id=1, source_target_pairs={{0,2},{1,3},{2,4},{3,5},{4,6},{5,7},{6,0},{7,1},{8,10},{9,11},{10,... | collective-permute-start | bytes 442376 | tf_op jit(solution)/shard_map/ppermute | solution.py:311
  188.3 40.9 %collective-permute-start.32 = (bf16[512,1152]{1,0:T(8,128)(2,1)S(1)}, bf16[512,1152]{1,0:T(8,128)(2,1)S(1)}, u32[]{:S(2)}, u32[]{:S(2)}) collective-permute-start(bf16[512,1152]{1,0:T(8,128)(2,1)S(1)} %pad_maximum_fusion.refs_4_.refs_6_), channel_id=1, source_target_pairs={{0,32},{16,48},{32,0},{48,16},{64,96},{80,112},{96,64},{112,80},{1... | collective-permute-start | bytes 3538952 | tf_op jit(solution)/shard_map/ppermute | solution.py:302
  189.9 8.7 %collective-permute-start.37 = (bf16[64,1152]{1,0:T(8,128)(2,1)S(1)}, bf16[64,1152]{1,0:T(8,128)(2,1)S(1)}, u32[]{:S(2)}, u32[]{:S(2)}) collective-permute-start(bf16[64,1152]{1,0:T(8,128)(2,1)S(1)} %fusion.5.refs_0_), channel_id=1, source_target_pairs={{0,6},{1,7},{2,0},{3,1},{4,2},{5,3},{6,4},{7,5},{8,14},{9,15},{10,... | collective-permute-start | bytes 442376 | tf_op jit(solution)/shard_map/ppermute | solution.py:311
  191.9 11.2 %collective-permute-start.27 = (bf16[64,1152]{1,0:T(8,128)(2,1)S(1)}, bf16[64,1152]{1,0:T(8,128)(2,1)S(1)}, u32[]{:S(2)}, u32[]{:S(2)}) collective-permute-start(bf16[64,1152]{1,0:T(8,128)(2,1)S(1)} %collective-permute-done.26.refs_0_), channel_id=1, source_target_pairs={{0,2},{1,3},{2,4},{3,5},{4,6},{5,7},{6,0},{7,1},{8,10},{9,11},{10,... | collective-permute-start | bytes 442376 | tf_op jit(solution)/shard_map/ppermute | solution.py:311
  198.7 23.4 %collective-permute-start.39 = (bf16[128,1152]{1,0:T(8,128)(2,1)S(1)}, bf16[128,1152]{1,0:T(8,128)(2,1)S(1)}, u32[]{:S(2)}, u32[]{:S(2)}) collective-permute-start(bf16[128,1152]{1,0:T(8,128)(2,1)S(1)} %constant_dynamic-update-slice_fusion.6), channel_id=1, source_target_pairs={{0,1},{1,2},{2,3},{3,4},{4,5},{5,6},{6,7},{7,0},{8,9},{9,10},{10,1... | collective-permute-start | bytes 884744 | tf_op jit(solution)/shard_map/ppermute | solution.py:296
  202.2 23.1 %collective-permute-start.40 = (bf16[128,1152]{1,0:T(8,128)(2,1)S(1)}, bf16[128,1152]{1,0:T(8,128)(2,1)S(1)}, u32[]{:S(2)}, u32[]{:S(2)}) collective-permute-start(bf16[128,1152]{1,0:T(8,128)(2,1)S(1)} %constant_dynamic-update-slice_fusion.6), channel_id=1, source_target_pairs={{0,7},{1,0},{2,1},{3,2},{4,3},{5,4},{6,5},{7,6},{8,15},{9,8},{10,9... | collective-permute-start | bytes 884744 | tf_op jit(solution)/shard_map/ppermute | solution.py:296
  203.1 9.7 %collective-permute-start.28 = (bf16[64,1152]{1,0:T(8,128)(2,1)S(1)}, bf16[64,1152]{1,0:T(8,128)(2,1)S(1)}, u32[]{:S(2)}, u32[]{:S(2)}) collective-permute-start(bf16[64,1152]{1,0:T(8,128)(2,1)S(1)} %collective-permute-done.26.refs_0_), channel_id=1, source_target_pairs={{0,6},{1,7},{2,0},{3,1},{4,2},{5,3},{6,4},{7,5},{8,14},{9,15},{10,... | collective-permute-start | bytes 442376 | tf_op jit(solution)/shard_map/ppermute | solution.py:311
  212.8 9.3 %collective-permute-start.38 = (bf16[64,1152]{1,0:T(8,128)(2,1)S(1)}, bf16[64,1152]{1,0:T(8,128)(2,1)S(1)}, u32[]{:S(2)}, u32[]{:S(2)}) collective-permute-start(bf16[64,1152]{1,0:T(8,128)(2,1)S(1)} %collective-permute-done.36.refs_1_), channel_id=1, source_target_pairs={{0,2},{1,3},{2,4},{3,5},{4,6},{5,7},{6,0},{7,1},{8,10},{9,11},{10,... | collective-permute-start | bytes 442376 | tf_op jit(solution)/shard_map/ppermute | solution.py:311
  222.1 11.7 %collective-permute-start.30 = (bf16[128,1152]{1,0:T(8,128)(2,1)S(1)}, bf16[128,1152]{1,0:T(8,128)(2,1)S(1)}, u32[]{:S(2)}, u32[]{:S(2)}) collective-permute-start(bf16[128,1152]{1,0:T(8,128)(2,1)S(1)} %constant_dynamic-update-slice_fusion.4), channel_id=1, source_target_pairs={{0,1},{1,2},{2,3},{3,4},{4,5},{5,6},{6,7},{7,0},{8,9},{9,10},{10,1... | collective-permute-start | bytes 884744 | tf_op jit(solution)/shard_map/ppermute | solution.py:296
  222.1 11.7 %collective-permute-start.31 = (bf16[128,1152]{1,0:T(8,128)(2,1)S(1)}, bf16[128,1152]{1,0:T(8,128)(2,1)S(1)}, u32[]{:S(2)}, u32[]{:S(2)}) collective-permute-start(bf16[128,1152]{1,0:T(8,128)(2,1)S(1)} %constant_dynamic-update-slice_fusion.4), channel_id=1, source_target_pairs={{0,7},{1,0},{2,1},{3,2},{4,3},{5,4},{6,5},{7,6},{8,15},{9,8},{10,9... | collective-permute-start | bytes 884744 | tf_op jit(solution)/shard_map/ppermute | solution.py:296
  225.3 8.4 %collective-permute-start.29 = (bf16[64,1152]{1,0:T(8,128)(2,1)S(1)}, bf16[64,1152]{1,0:T(8,128)(2,1)S(1)}, u32[]{:S(2)}, u32[]{:S(2)}) collective-permute-start(bf16[64,1152]{1,0:T(8,128)(2,1)S(1)} %collective-permute-done.27.refs_1_), channel_id=1, source_target_pairs={{0,2},{1,3},{2,4},{3,5},{4,6},{5,7},{6,0},{7,1},{8,10},{9,11},{10,... | collective-permute-start | bytes 442376 | tf_op jit(solution)/shard_map/ppermute | solution.py:311

commit v2 on v1

--- a/solution.py
+++ b/solution.py
@@ -63,8 +63,15 @@
     k = 0
     for ref in refs:
         for i in range(ref.shape[0] // pair):
-            for start, offset, size in pieces(k, pair, paired, total):
-                target[start : start + size, :] = ref[i * pair + offset : i * pair + offset + size, :]
+
+            def copy(part, ref=ref, i=i, k=k):
+                for start, offset, size in pieces(k, pair, paired, total):
+                    for at in range(0, size, pair // 2):
+                        source = pl.ds(pl.multiple_of(i * pair + offset + at + part, PART), PART)
+                        here = pl.ds(pl.multiple_of(start + at + part, PART), PART)
+                        target[here, :] = ref[source, :]
+
+            each_part(pair // 2, PART, copy)
             k += 1
 
 
@@ -116,17 +123,17 @@
 
 def cast_body(gate, up, down, stacked, halves):
     def one(start):
-        here = pl.ds(start, UNITS)
+        here = pl.ds(start, PART)
         for i, ref in enumerate((gate, up, down)):
             stacked[i, here, :] = ref[here, :]
             halves[i, here, :] = ref[here, :].astype(BF16)
 
-    each_part(gate.shape[0], UNITS, one)
+    each_part(gate.shape[0], PART, one)
 
 
 def mean_body(mine, near, base):
-    for i in range(3):
-
+    @pl.loop(0, 3)
+    def _(i):
         @pl.loop(0, mine.shape[1] // UNITS)
         def _(step):
             here = pl.ds(pl.multiple_of(step * UNITS, UNITS), UNITS)
@@ -142,8 +149,18 @@
     k = 0
     for ref in blocks:
         for i in range(ref.shape[0] // size):
-            x[k * pair : (k + 1) * pair, :] = ref[i * size : i * size + pair, :]
-            column[k * rows : (k + 1) * rows, :] = ref[i * size + pair : (i + 1) * size, :]
+
+            def copy(part, ref=ref, i=i, k=k):
+                for at, target, start in (
+                    (0, x, k * pair),
+                    (rows, x, k * pair + rows),
+                    (pair, column, k * rows),
+                ):
+                    source = pl.ds(pl.multiple_of(i * size + at + part, PART), PART)
+                    here = pl.ds(pl.multiple_of(start + part, PART), PART)
+                    target[here, :] = ref[source, :]
+
+            each_part(rows, PART, copy)
             k += 1
     column[k * rows : (k + 1) * rows, :] = targets[0]
     column[(k + 1) * rows :, :] = targets[1]
@@ -197,8 +214,8 @@
     offset = core[0] * (halves.shape[1] - size)
     weights, act, slope, hidden, down = kept
 
-    for i in range(3):
-
+    @pl.loop(0, 3)
+    def _(i):
         @pl.loop(0, base.shape[1] // UNITS)
         def _(step):
             here = pl.ds(pl.multiple_of(step * UNITS, UNITS), UNITS)
@@ -211,7 +228,7 @@
     partial_into(hidden, halves.at[2], partials, pair, False, turned)
 
     def keep(start):
-        down[pl.ds(start, UNITS), :] = halves[2, pl.ds(start, UNITS), :]
+        down[pl.ds(start, PART), :] = halves[2, pl.ds(start, PART), :]
 
     def send(start):
         source = pl.ds(pl.multiple_of(offset + start, PART), PART)
@@ -224,7 +241,7 @@
         source = pl.ds(pl.multiple_of(offset + size // 2 + start, PART), PART)
         sent_out[pl.ds(start, PART), :] = halves[1, source, :]
 
-    each_part(down.shape[0], UNITS, keep)
+    each_part(down.shape[0], PART, keep)
     each_part(size, PART, send)
     each_part(size // 2, PART, send_half)
 

time: 241 us -> 241 us (level)
    ppermute x18, waiting for transfers between devices: 75.5 us -> 73 us  [two_along(): return lax.ppermute(value, ('rep', 'hid'), pairs)]
where the time goes in v2:
time: 241 us; the launch traced here: 239 us
  waiting for transfers between devices  121 us (50%)
  starting transfers between devices  73.4 us (30%)
  Pallas kernels  35.1 us (15%)
  local copies, waits for them, and re-layouts  7.87 us (3%)
    ppermute x18, waiting for transfers between devices, two_along(): return lax.ppermute(value, ('rep', 'hid'), pairs)  73 us
    ppermute x4, waiting for transfers between devices, across_y(): return lax.ppermute(value, 'hid', [(h, h ^ n_z) for h in range(n_hid)])  46.4 us
    ppermute x18, starting transfers between devices, two_along(): return lax.ppermute(value, ('rep', 'hid'), pairs)  35.9 us
    pallas_call x9, Pallas kernels, kernel_call(): pl.pallas_call(body, out_shape=out_shape, in_specs=[VMEM_SPEC] * len(args...  35.1 us
    ppermute x12, starting transfers between devices, along_z(): return lax.ppermute(value, 'hid', pairs)  22.4 us
    ppermute x7, starting transfers between devices, with_replica(): return lax.ppermute(value, 'rep', [(r, r ^ mask) for r in range(n_rep)])  8.51 us
    ppermute x4, starting transfers between devices, across_y(): return lax.ppermute(value, 'hid', [(h, h ^ n_z) for h in range(n_hid)])  6.51 us
    unnamed x16, local copies, waits for them, and re-layouts  5.55 us
  transfers between devices with their start and end apart: 41, of which 21 were waited for; matrix products, arithmetic and copies ran while one was open for 1% of the time, Pallas kernels for 8%

profile of v2, /device:TPU:2, one launch (start us, length us, event | category | flops | bytes accessed | tf_op | source)
XLA Modules:
  0.0 239.0 jit_solution(9313545872044189591)
XLA Ops:
  0.6 0.9 slice_bitcast_fusion.3
  1.6 1.7 collective-permute-start.1
  3.2 2.8 %collective-permute-done.1 = bf16[32,1152]{1,0:T(8,128)(2,1)S(1)} collective-permute-done((bf16[32,1152]{1,0:T(8,128)(2,1)S(1)}, bf16[32,1152]{1,0:T(8,128)(2,1)S(1)}, u32[]{:S(2)}, u32[]{:S(2)}) %collective-permute-start.1) | collective-permute-done | bytes 73760 | tf_op jit(solution)/shard_map/ppermute | solution.py:316
  6.0 3.3 %collective-permute-start.2 = (bf16[96,1152]{1,0:T(8,128)(2,1)S(1)}, bf16[96,1152]{1,0:T(8,128)(2,1)S(1)}, u32[]{:S(2)}, u32[]{:S(2)}) collective-permute-start(bf16[96,1152]{1,0:T(8,128)(2,1)S(1)} %pad_maximum_fusion.1.refs_0_), channel_id=1, source_target_pairs={{0,2},{1,3},{2,4},{3,5},{4,6},{5,7},{6,0},{7,1},{8,10},{9,11},{10,... | collective-permute-start | bytes 663560 | tf_op jit(solution)/shard_map/ppermute | solution.py:328
  9.4 3.1 %collective-permute-start.3 = (bf16[96,1152]{1,0:T(8,128)(2,1)S(1)}, bf16[96,1152]{1,0:T(8,128)(2,1)S(1)}, u32[]{:S(2)}, u32[]{:S(2)}) collective-permute-start(bf16[96,1152]{1,0:T(8,128)(2,1)S(1)} %pad_maximum_fusion.1.refs_0_), channel_id=1, source_target_pairs={{0,6},{1,7},{2,0},{3,1},{4,2},{5,3},{6,4},{7,5},{8,14},{9,15},{10,... | collective-permute-start | bytes 663560 | tf_op jit(solution)/shard_map/ppermute | solution.py:328
  12.5 6.0 %collective-permute-done.2.refs_1_ = bf16[96,1152]{1,0:T(8,128)(2,1)S(1)} collective-permute-done((bf16[96,1152]{1,0:T(8,128)(2,1)S(1)}, bf16[96,1152]{1,0:T(8,128)(2,1)S(1)}, u32[]{:S(2)}, u32[]{:S(2)}) %collective-permute-start.2) | collective-permute-done | bytes 221216 | tf_op jit(solution)/shard_map/ppermute | solution.py:328
  18.5 2.2 collective-permute-done.3.refs_2_
  20.7 3.2 %collective-permute-start.5 = (bf16[192,1152]{1,0:T(8,128)(2,1)S(1)}, bf16[192,1152]{1,0:T(8,128)(2,1)S(1)}, u32[]{:S(2)}, u32[]{:S(2)}) collective-permute-start(bf16[192,1152]{1,0:T(8,128)(2,1)S(1)} %constant_dynamic-update-slice_fusion), channel_id=1, source_target_pairs={{0,1},{1,2},{2,3},{3,4},{4,5},{5,6},{6,7},{7,0},{8,9},{9,10},{10,1... | collective-permute-start | bytes 1327112 | tf_op jit(solution)/shard_map/ppermute | solution.py:313
  23.9 1.1 collective-permute-start.6
  25.0 1.2 collective-permute-start.4
  26.2 1.6 copy-done
  27.8 1.6 copy-done.1
  29.3 1.6 copy-done.2
  30.9 3.2 %shard_map.76 = (f32[3,432,1152]{2,1,0:T(8,128)}, bf16[3,432,1152]{2,1,0:T(8,128)(2,1)S(1)}) custom-call(f32[432,1152]{1,0:T(8,128)S(1)} %bitcast.12, f32[432,1152]{1,0:T(8,128)S(1)} %bitcast.13, f32[432,1152]{1,0:T(8,128)S(1)} %bitcast.14), custom_call_target="tpu_custom_call" | custom-call | bytes 14929920 | tf_op jit(solution)/shard_map/pallas_call | solution.py:42
  34.1 6.6 %collective-permute-done.4.refs_3_ = bf16[96,1152]{1,0:T(8,128)(2,1)S(1)} collective-permute-done((bf16[96,1152]{1,0:T(8,128)(2,1)S(1)}, bf16[96,1152]{1,0:T(8,128)(2,1)S(1)}, u32[]{:S(2)}, u32[]{:S(2)}) %collective-permute-start.4) | collective-permute-done | bytes 221216 | tf_op jit(solution)/shard_map/ppermute | solution.py:328
  40.7 3.8 %shard_map.78 = (bf16[512,1152]{1,0:T(8,128)(2,1)S(1)}, bf16[320,1152]{1,0:T(8,128)(2,1)S(1)}, f32[432,512]{1,0:T(8,128)S(1)}, f32[432,512]{1,0:T(8,128)S(1)}, b...) custom-call(bf16[96,1152]{1,0:T(8,128)(2,1)S(1)} %pad_maximum_fusion, ...), custom_call_target="tpu_custom_call" | custom-call | flops 1528823808 | bytes 10211328 | tf_op jit(solution)/shard_map/pallas_call | solution.py:42
  44.7 3.2 %collective-permute-start.7 = (bf16[128,1152]{1,0:T(8,128)(2,1)S(1)}, bf16[128,1152]{1,0:T(8,128)(2,1)S(1)}, u32[]{:S(2)}, u32[]{:S(2)}) collective-permute-start(bf16[128,1152]{1,0:T(8,128)(2,1)S(1)} %get-tuple-element.37), channel_id=1, source_target_pairs={{0,7},{1,0},{2,1},{3,2},{4,3},{5,4},{6,5},{7,6},{8,15},{9,8},{10,9... | collective-permute-start | bytes 884744 | tf_op jit(solution)/shard_map/ppermute | solution.py:313
  48.6 9.6 %collective-permute-done.9 = bf16[64,1152]{1,0:T(8,128)(2,1)S(1)} collective-permute-done((bf16[64,1152]{1,0:T(8,128)(2,1)S(1)}, bf16[64,1152]{1,0:T(8,128)(2,1)S(1)}, u32[]{:S(2)}, u32[]{:S(2)}) %collective-permute-start.9) | collective-permute-done | bytes 147488 | tf_op jit(solution)/shard_map/ppermute | solution.py:328
  58.3 2.8 %collective-permute-start.11 = (bf16[64,1152]{1,0:T(8,128)(2,1)S(1)}, bf16[64,1152]{1,0:T(8,128)(2,1)S(1)}, u32[]{:S(2)}, u32[]{:S(2)}) collective-permute-start(bf16[64,1152]{1,0:T(8,128)(2,1)S(1)} %get-tuple-element.68), channel_id=1, source_target_pairs={{0,2},{1,3},{2,4},{3,5},{4,6},{5,7},{6,0},{7,1},{8,10},{9,11},{10,... | collective-permute-start | bytes 442376 | tf_op jit(solution)/shard_map/ppermute | solution.py:328
  61.2 1.4 collective-permute-start.10
  62.6 1.6 collective-permute-start.13
  64.1 2.9 %collective-permute-done.11 = bf16[64,1152]{1,0:T(8,128)(2,1)S(1)} collective-permute-done((bf16[64,1152]{1,0:T(8,128)(2,1)S(1)}, bf16[64,1152]{1,0:T(8,128)(2,1)S(1)}, u32[]{:S(2)}, u32[]{:S(2)}) %collective-permute-start.11) | collective-permute-done | bytes 147488 | tf_op jit(solution)/shard_map/ppermute | solution.py:328
  67.9 1.6 collective-permute-start.12
  69.6 15.1 %collective-permute-done.12 = bf16[64,1152]{1,0:T(8,128)(2,1)S(1)} collective-permute-done((bf16[64,1152]{1,0:T(8,128)(2,1)S(1)}, bf16[64,1152]{1,0:T(8,128)(2,1)S(1)}, u32[]{:S(2)}, u32[]{:S(2)}) %collective-permute-start.12) | collective-permute-done | bytes 147488 | tf_op jit(solution)/shard_map/ppermute | solution.py:316
  85.6 1.8 collective-permute-start.14
  87.4 2.6 %collective-permute-start.15 = (bf16[64,1152]{1,0:T(8,128)(2,1)S(1)}, bf16[64,1152]{1,0:T(8,128)(2,1)S(1)}, u32[]{:S(2)}, u32[]{:S(2)}) collective-permute-start(bf16[64,1152]{1,0:T(8,128)(2,1)S(1)} %fusion.2.refs_0_), channel_id=1, source_target_pairs={{0,6},{1,7},{2,0},{3,1},{4,2},{5,3},{6,4},{7,5},{8,14},{9,15},{10,... | collective-permute-start | bytes 442376 | tf_op jit(solution)/shard_map/ppermute | solution.py:328
  90.0 5.5 %collective-permute-done.14.refs_1_ = bf16[64,1152]{1,0:T(8,128)(2,1)S(1)} collective-permute-done((bf16[64,1152]{1,0:T(8,128)(2,1)S(1)}, bf16[64,1152]{1,0:T(8,128)(2,1)S(1)}, u32[]{:S(2)}, u32[]{:S(2)}) %collective-permute-start.14) | collective-permute-done | bytes 147488 | tf_op jit(solution)/shard_map/ppermute | solution.py:328
  95.6 2.1 collective-permute-start.17
  97.7 1.2 collective-permute-start.18
  98.9 1.1 collective-permute-start.16
  100.0 7.2 %collective-permute-done.16.refs_3_ = bf16[64,1152]{1,0:T(8,128)(2,1)S(1)} collective-permute-done((bf16[64,1152]{1,0:T(8,128)(2,1)S(1)}, bf16[64,1152]{1,0:T(8,128)(2,1)S(1)}, u32[]{:S(2)}, u32[]{:S(2)}) %collective-permute-start.16) | collective-permute-done | bytes 147488 | tf_op jit(solution)/shard_map/ppermute | solution.py:328
  107.6 1.0 collective-permute-done.18.refs_5_
  108.5 3.7 %shard_map.79.refs_2_ = bf16[3,432,1152]{2,1,0:T(8,128)(2,1)S(1)} custom-call(bf16[64,1152]{1,0:T(8,128)(2,1)S(1)} %fusion.2.refs_0_, bf16[64,1152]{1,0:T(8,128)(2,1)S(1)} %collective-permute-done.14.refs_1_, bf16[64,1152]{1,0:T(8,128)(2,1)S(1)} %collective-permute-done.15.refs_2_, bf16[64,1152]{1,0:T(8,128)(2,1)S(1)} %collective-permute-done.16.refs_3_, ...), custom_call_target="tpu_custom_call" | custom-call | flops 2038431744 | bytes 10543104 | tf_op jit(solution)/shard_map/pallas_call | solution.py:42
  112.3 1.0 collective-permute-start.19
  113.3 1.2 slice.71
  114.6 5.3 %shard_map.77.refs_1_ = f32[3,432,1152]{2,1,0:T(8,128)S(1)} custom-call(f32[3,432,1152]{2,1,0:T(8,128)} %get-tuple-element.33.mine, f32[3,432,1152]{2,1,0:T(8,128)} %collective-permute-done.near), custom_call_target="tpu_custom_call" | custom-call | bytes 17915904 | tf_op jit(solution)/shard_map/pallas_call | solution.py:42
  119.9 7.3 %shard_map.80 = (f32[3,432,1152]{2,1,0:T(8,128)S(1)}, f32[432,512]{1,0:T(8,128)S(1)}, f32[432,512]{1,0:T(8,128)S(1)}, bf16[432,512]{1,0:T(8,128)(2,1)S(1)}, bf16...) custom-call(s32[1]{0:T(128)} %bitcast.refs_0_.core, ...), custom_call_target="tpu_custom_call" | custom-call | flops 1528823808 | bytes 25030660 | tf_op jit(solution)/shard_map/pallas_call | solution.py:42
  127.2 1.3 collective-permute-start.21
  128.5 2.0 collective-permute-start.20
  130.5 2.2 collective-permute-start.22
  132.7 9.4 %collective-permute-done.22 = bf16[64,1152]{1,0:T(8,128)(2,1)S(1)} collective-permute-done((bf16[64,1152]{1,0:T(8,128)(2,1)S(1)}, bf16[64,1152]{1,0:T(8,128)(2,1)S(1)}, u32[]{:S(2)}, u32[]{:S(2)}) %collective-permute-start.22) | collective-permute-done | bytes 147488 | tf_op jit(solution)/shard_map/ppermute | solution.py:328
  142.2 1.9 collective-permute-start.24
  144.1 2.3 collective-permute-start.23
  146.5 3.2 %collective-permute-start.33 = (bf16[336,1152]{1,0:T(8,128)(2,1)S(1)}, bf16[336,1152]{1,0:T(8,128)(2,1)S(1)}, u32[]{:S(2)}, u32[]{:S(2)}) collective-permute-start(bf16[336,1152]{1,0:T(8,128)(2,1)S(1)} %get-tuple-element.52), channel_id=1, source_target_pairs={{0,32},{16,48},{32,0},{48,16},{64,96},{80,112},{96,64},{112,80},{1... | collective-permute-start | bytes 2322440 | tf_op jit(solution)/shard_map/ppermute | solution.py:319
  150.0 3.4 %collective-permute-done.24 = bf16[64,1152]{1,0:T(8,128)(2,1)S(1)} collective-permute-done((bf16[64,1152]{1,0:T(8,128)(2,1)S(1)}, bf16[64,1152]{1,0:T(8,128)(2,1)S(1)}, u32[]{:S(2)}, u32[]{:S(2)}) %collective-permute-start.24) | collective-permute-done | bytes 147488 | tf_op jit(solution)/shard_map/ppermute | solution.py:328
  153.4 1.6 collective-permute-start.25
  155.0 28.5 %collective-permute-done.25 = bf16[64,1152]{1,0:T(8,128)(2,1)S(1)} collective-permute-done((bf16[64,1152]{1,0:T(8,128)(2,1)S(1)}, bf16[64,1152]{1,0:T(8,128)(2,1)S(1)}, u32[]{:S(2)}, u32[]{:S(2)}) %collective-permute-start.25) | collective-permute-done | bytes 147488 | tf_op jit(solution)/shard_map/ppermute | solution.py:316
  184.2 1.9 collective-permute-start.26
  186.2 2.2 collective-permute-start.36
  188.4 1.7 collective-permute-start.32
  190.1 1.9 collective-permute-start.37
  192.1 2.7 %collective-permute-start.27 = (bf16[64,1152]{1,0:T(8,128)(2,1)S(1)}, bf16[64,1152]{1,0:T(8,128)(2,1)S(1)}, u32[]{:S(2)}, u32[]{:S(2)}) collective-permute-start(bf16[64,1152]{1,0:T(8,128)(2,1)S(1)} %collective-permute-done.26.refs_0_), channel_id=1, source_target_pairs={{0,2},{1,3},{2,4},{3,5},{4,6},{5,7},{6,0},{7,1},{8,10},{9,11},{10,... | collective-permute-start | bytes 442376 | tf_op jit(solution)/shard_map/ppermute | solution.py:328
  194.8 4.0 %collective-permute-done.37.refs_2_ = bf16[64,1152]{1,0:T(8,128)(2,1)S(1)} collective-permute-done((bf16[64,1152]{1,0:T(8,128)(2,1)S(1)}, bf16[64,1152]{1,0:T(8,128)(2,1)S(1)}, u32[]{:S(2)}, u32[]{:S(2)}) %collective-permute-start.37) | collective-permute-done | bytes 147488 | tf_op jit(solution)/shard_map/ppermute | solution.py:328
  198.8 3.6 %collective-permute-start.39 = (bf16[128,1152]{1,0:T(8,128)(2,1)S(1)}, bf16[128,1152]{1,0:T(8,128)(2,1)S(1)}, u32[]{:S(2)}, u32[]{:S(2)}) collective-permute-start(bf16[128,1152]{1,0:T(8,128)(2,1)S(1)} %constant_dynamic-update-slice_fusion.6), channel_id=1, source_target_pairs={{0,1},{1,2},{2,3},{3,4},{4,5},{5,6},{6,7},{7,0},{8,9},{9,10},{10,1... | collective-permute-start | bytes 884744 | tf_op jit(solution)/shard_map/ppermute | solution.py:313
  203.3 2.4 %collective-permute-start.28 = (bf16[64,1152]{1,0:T(8,128)(2,1)S(1)}, bf16[64,1152]{1,0:T(8,128)(2,1)S(1)}, u32[]{:S(2)}, u32[]{:S(2)}) collective-permute-start(bf16[64,1152]{1,0:T(8,128)(2,1)S(1)} %collective-permute-done.26.refs_0_), channel_id=1, source_target_pairs={{0,6},{1,7},{2,0},{3,1},{4,2},{5,3},{6,4},{7,5},{8,14},{9,15},{10,... | collective-permute-start | bytes 442376 | tf_op jit(solution)/shard_map/ppermute | solution.py:328
  205.8 6.7 %collective-permute-done.28.refs_2_ = bf16[64,1152]{1,0:T(8,128)(2,1)S(1)} collective-permute-done((bf16[64,1152]{1,0:T(8,128)(2,1)S(1)}, bf16[64,1152]{1,0:T(8,128)(2,1)S(1)}, u32[]{:S(2)}, u32[]{:S(2)}) %collective-permute-start.28) | collective-permute-done | bytes 147488 | tf_op jit(solution)/shard_map/ppermute | solution.py:328
  212.5 2.1 collective-permute-start.38
  214.6 5.2 %collective-permute-done.38.refs_3_ = bf16[64,1152]{1,0:T(8,128)(2,1)S(1)} collective-permute-done((bf16[64,1152]{1,0:T(8,128)(2,1)S(1)}, bf16[64,1152]{1,0:T(8,128)(2,1)S(1)}, u32[]{:S(2)}, u32[]{:S(2)}) %collective-permute-start.38) | collective-permute-done | bytes 147488 | tf_op jit(solution)/shard_map/ppermute | solution.py:328
  219.8 2.9 %collective-permute-start.30 = (bf16[128,1152]{1,0:T(8,128)(2,1)S(1)}, bf16[128,1152]{1,0:T(8,128)(2,1)S(1)}, u32[]{:S(2)}, u32[]{:S(2)}) collective-permute-start(bf16[128,1152]{1,0:T(8,128)(2,1)S(1)} %constant_dynamic-update-slice_fusion.4), channel_id=1, source_target_pairs={{0,1},{1,2},{2,3},{3,4},{4,5},{5,6},{6,7},{7,0},{8,9},{9,10},{10,1... | collective-permute-start | bytes 884744 | tf_op jit(solution)/shard_map/ppermute | solution.py:313
  222.8 1.5 collective-permute-start.31
  224.3 3.9 %shard_map.83.refs_11_ = f32[3,432,1152]{2,1,0:T(8,128)S(1)} custom-call(bf16[64,1152]{1,0:T(8,128)(2,1)S(1)} %fusion.5.refs_0_, bf16[64,1152]{1,0:T(8,128)(2,1)S(1)} %collective-permute-done.36.refs_1_, bf16[64,1152]{1,0:T(8,128)(2,1)S(1)} %collective-permute-done.37.refs_2_, bf16[64,1152]{1,0:T(8,128)(2,1)S(1)} %collective-permute-done.38.refs_3_, ...), custom_call_target="tpu_custom_call" | custom-call | flops 2038431744 | bytes 17510400 | tf_op jit(solution)/shard_map/pallas_call | solution.py:42
  228.2 2.5 %shard_map.82 = (bf16[3,432,1152]{2,1,0:T(8,128)(2,1)S(1)}, f32[432,512]{1,0:T(8,128)S(1)}, f32[432,512]{1,0:T(8,128)S(1)}, bf16[432,512]{1,0:T(8,128)(2,1)S(1)}) custom-call(s32[1]{0:T(128)} %bitcast.refs_0_.core, bf16[512,1152]{1,0:T(8,128)(2,1)S(1)} %collective-permute-done.32.x.refs_6_, bf16[672,1152]{1,0:T(8,128)(2,1)S(1)} %shard_map.81.direct, ...), custom_call_target="tpu_custom_call" | custom-call | flops 1019215872 | bytes 9474052 | tf_op jit(solution)/shard_map/pallas_call | solution.py:42
  230.6 2.9 %collective-permute-done.29.refs_3_ = bf16[64,1152]{1,0:T(8,128)(2,1)S(1)} collective-permute-done((bf16[64,1152]{1,0:T(8,128)(2,1)S(1)}, bf16[64,1152]{1,0:T(8,128)(2,1)S(1)}, u32[]{:S(2)}, u32[]{:S(2)}) %collective-permute-start.29) | collective-permute-done | bytes 147488 | tf_op jit(solution)/shard_map/ppermute | solution.py:328
  233.6 5.2 %shard_map.84 = (f32[1,432,1152]{2,1,0:T(8,128)}, f32[1,432,1152]{2,1,0:T(8,128)}, f32[1,432,1152]{2,1,0:T(8,128)}) custom-call(bf16[64,1152]{1,0:T(8,128)(2,1)S(1)} %collective-permute-done.26.refs_0_, bf16[64,1152]{1,0:T(8,128)(2,1)S(1)} %collective-permute-done.27.refs_1_, bf16[64,1152]{1,0:T(8,128)(2,1)S(1)} %collective-permute-done.28.refs_2_, ...), custom_call_target="tpu_custom_call" | custom-call | flops 2038431744 | bytes 19501056 | tf_op jit(solution)/shard_map/pallas_call | solution.py:42
  (63 shorter events, 5.6 us)
Async XLA Ops:
  1.6 4.4 %collective-permute-start.1 = (bf16[32,1152]{1,0:T(8,128)(2,1)S(1)}, bf16[32,1152]{1,0:T(8,128)(2,1)S(1)}, u32[]{:S(2)}, u32[]{:S(2)}) collective-permute-start(bf16[32,1152]{1,0:T(8,128)(2,1)S(1)} %get-tuple-element.75), channel_id=1, source_target_pairs={{0,8},{1,9},{2,10},{3,11},{4,12},{5,13},{6,14},{7,15},{8,0},{9,1},... | collective-permute-start | bytes 221192 | tf_op jit(solution)/shard_map/ppermute | solution.py:316
  6.0 12.5 %collective-permute-start.2 = (bf16[96,1152]{1,0:T(8,128)(2,1)S(1)}, bf16[96,1152]{1,0:T(8,128)(2,1)S(1)}, u32[]{:S(2)}, u32[]{:S(2)}) collective-permute-start(bf16[96,1152]{1,0:T(8,128)(2,1)S(1)} %pad_maximum_fusion.1.refs_0_), channel_id=1, source_target_pairs={{0,2},{1,3},{2,4},{3,5},{4,6},{5,7},{6,0},{7,1},{8,10},{9,11},{10,... | collective-permute-start | bytes 663560 | tf_op jit(solution)/shard_map/ppermute | solution.py:328
  9.4 11.3 %collective-permute-start.3 = (bf16[96,1152]{1,0:T(8,128)(2,1)S(1)}, bf16[96,1152]{1,0:T(8,128)(2,1)S(1)}, u32[]{:S(2)}, u32[]{:S(2)}) collective-permute-start(bf16[96,1152]{1,0:T(8,128)(2,1)S(1)} %pad_maximum_fusion.1.refs_0_), channel_id=1, source_target_pairs={{0,6},{1,7},{2,0},{3,1},{4,2},{5,3},{6,4},{7,5},{8,14},{9,15},{10,... | collective-permute-start | bytes 663560 | tf_op jit(solution)/shard_map/ppermute | solution.py:328
  20.7 20.0 %collective-permute-start.5 = (bf16[192,1152]{1,0:T(8,128)(2,1)S(1)}, bf16[192,1152]{1,0:T(8,128)(2,1)S(1)}, u32[]{:S(2)}, u32[]{:S(2)}) collective-permute-start(bf16[192,1152]{1,0:T(8,128)(2,1)S(1)} %constant_dynamic-update-slice_fusion), channel_id=1, source_target_pairs={{0,1},{1,2},{2,3},{3,4},{4,5},{5,6},{6,7},{7,0},{8,9},{9,10},{10,1... | collective-permute-start | bytes 1327112 | tf_op jit(solution)/shard_map/ppermute | solution.py:313
  23.9 16.8 %collective-permute-start.6 = (bf16[192,1152]{1,0:T(8,128)(2,1)S(1)}, bf16[192,1152]{1,0:T(8,128)(2,1)S(1)}, u32[]{:S(2)}, u32[]{:S(2)}) collective-permute-start(bf16[192,1152]{1,0:T(8,128)(2,1)S(1)} %constant_dynamic-update-slice_fusion), channel_id=1, source_target_pairs={{0,7},{1,0},{2,1},{3,2},{4,3},{5,4},{6,5},{7,6},{8,15},{9,8},{10,9... | collective-permute-start | bytes 1327112 | tf_op jit(solution)/shard_map/ppermute | solution.py:313
  25.0 15.7 %collective-permute-start.4 = (bf16[96,1152]{1,0:T(8,128)(2,1)S(1)}, bf16[96,1152]{1,0:T(8,128)(2,1)S(1)}, u32[]{:S(2)}, u32[]{:S(2)}) collective-permute-start(bf16[96,1152]{1,0:T(8,128)(2,1)S(1)} %collective-permute-done.2.refs_1_), channel_id=1, source_target_pairs={{0,2},{1,3},{2,4},{3,5},{4,6},{5,7},{6,0},{7,1},{8,10},{9,11},{10,... | collective-permute-start | bytes 663560 | tf_op jit(solution)/shard_map/ppermute | solution.py:328
  26.2 1.6 copy-start
  27.8 1.6 copy-start.1
  29.3 1.6 copy-start.2
  30.9 9.8 %copy-start.4 = (bf16[2,32,1152]{2,1,0:T(8,128)(2,1)S(1)}, bf16[2,32,1152]{2,1,0:T(8,128)(2,1)}, u32[]{:S(2)}) copy-start(bf16[2,32,1152]{2,1,0:T(8,128)(2,1)} %refs_6_.1) | copy-start | bytes 442372
  44.6 40.1 %copy-start.3 = (bf16[320,1152]{1,0:T(8,128)(2,1)}, bf16[320,1152]{1,0:T(8,128)(2,1)S(1)}, u32[]{:S(2)}) copy-start(bf16[320,1152]{1,0:T(8,128)(2,1)S(1)} %get-tuple-element.41) | copy-start | bytes 2211844
  44.6 13.6 %collective-permute-start.8 = (bf16[128,1152]{1,0:T(8,128)(2,1)S(1)}, bf16[128,1152]{1,0:T(8,128)(2,1)S(1)}, u32[]{:S(2)}, u32[]{:S(2)}) collective-permute-start(bf16[128,1152]{1,0:T(8,128)(2,1)S(1)} %get-tuple-element.38), channel_id=1, source_target_pairs={{0,1},{1,2},{2,3},{3,4},{4,5},{5,6},{6,7},{7,0},{8,9},{9,10},{10,1... | collective-permute-start | bytes 884744 | tf_op jit(solution)/shard_map/ppermute | solution.py:313
  44.7 13.5 %collective-permute-start.7 = (bf16[128,1152]{1,0:T(8,128)(2,1)S(1)}, bf16[128,1152]{1,0:T(8,128)(2,1)S(1)}, u32[]{:S(2)}, u32[]{:S(2)}) collective-permute-start(bf16[128,1152]{1,0:T(8,128)(2,1)S(1)} %get-tuple-element.37), channel_id=1, source_target_pairs={{0,7},{1,0},{2,1},{3,2},{4,3},{5,4},{6,5},{7,6},{8,15},{9,8},{10,9... | collective-permute-start | bytes 884744 | tf_op jit(solution)/shard_map/ppermute | solution.py:313
  47.9 10.3 %collective-permute-start.9 = (bf16[64,1152]{1,0:T(8,128)(2,1)S(1)}, bf16[64,1152]{1,0:T(8,128)(2,1)S(1)}, u32[]{:S(2)}, u32[]{:S(2)}) collective-permute-start(bf16[64,1152]{1,0:T(8,128)(2,1)S(1)} %get-tuple-element.39), channel_id=1, source_target_pairs={{0,6},{1,7},{2,0},{3,1},{4,2},{5,3},{6,4},{7,5},{8,14},{9,15},{10,... | collective-permute-start | bytes 442376 | tf_op jit(solution)/shard_map/ppermute | solution.py:328
  58.3 8.7 %collective-permute-start.11 = (bf16[64,1152]{1,0:T(8,128)(2,1)S(1)}, bf16[64,1152]{1,0:T(8,128)(2,1)S(1)}, u32[]{:S(2)}, u32[]{:S(2)}) collective-permute-start(bf16[64,1152]{1,0:T(8,128)(2,1)S(1)} %get-tuple-element.68), channel_id=1, source_target_pairs={{0,2},{1,3},{2,4},{3,5},{4,6},{5,7},{6,0},{7,1},{8,10},{9,11},{10,... | collective-permute-start | bytes 442376 | tf_op jit(solution)/shard_map/ppermute | solution.py:328
  61.2 6.7 %collective-permute-start.10 = (bf16[64,1152]{1,0:T(8,128)(2,1)S(1)}, bf16[64,1152]{1,0:T(8,128)(2,1)S(1)}, u32[]{:S(2)}, u32[]{:S(2)}) collective-permute-start(bf16[64,1152]{1,0:T(8,128)(2,1)S(1)} %get-tuple-element.67), channel_id=1, source_target_pairs={{0,6},{1,7},{2,0},{3,1},{4,2},{5,3},{6,4},{7,5},{8,14},{9,15},{10,... | collective-permute-start | bytes 442376 | tf_op jit(solution)/shard_map/ppermute | solution.py:328
  62.6 52.1 %collective-permute-start = (f32[3,432,1152]{2,1,0:T(8,128)}, f32[3,432,1152]{2,1,0:T(8,128)}, u32[]{:S(2)}, u32[]{:S(2)}) collective-permute-start(f32[3,432,1152]{2,1,0:T(8,128)} %get-tuple-element.33.mine), channel_id=1, source_target_pairs={{0,16},{16,0},{32,48},{48,32},{64,80},{80,64},{96,112},{112,96},{1... | collective-permute-start | bytes 17915912 | tf_op jit(solution)/shard_map/ppermute | solution.py:319
  62.6 22.1 %collective-permute-start.13 = (bf16[320,1152]{1,0:T(8,128)(2,1)S(1)}, bf16[320,1152]{1,0:T(8,128)(2,1)S(1)}, u32[]{:S(2)}, u32[]{:S(2)}) collective-permute-start(bf16[320,1152]{1,0:T(8,128)(2,1)S(1)} %get-tuple-element.41), channel_id=1, source_target_pairs={{0,8},{1,9},{2,10},{3,11},{4,12},{5,13},{6,14},{7,15},{8,0},{9,1},... | collective-permute-start | bytes 2211848 | tf_op jit(solution)/shard_map/ppermute | solution.py:316
  67.9 16.7 %collective-permute-start.12 = (bf16[64,1152]{1,0:T(8,128)(2,1)S(1)}, bf16[64,1152]{1,0:T(8,128)(2,1)S(1)}, u32[]{:S(2)}, u32[]{:S(2)}) collective-permute-start(bf16[64,1152]{1,0:T(8,128)(2,1)S(1)} %fusion.6), channel_id=1, source_target_pairs={{0,8},{1,9},{2,10},{3,11},{4,12},{5,13},{6,14},{7,15},{8,0},{9,1},... | collective-permute-start | bytes 442376 | tf_op jit(solution)/shard_map/ppermute | solution.py:316
  84.7 0.9 copy-start.5
  85.6 9.9 %collective-permute-start.14 = (bf16[64,1152]{1,0:T(8,128)(2,1)S(1)}, bf16[64,1152]{1,0:T(8,128)(2,1)S(1)}, u32[]{:S(2)}, u32[]{:S(2)}) collective-permute-start(bf16[64,1152]{1,0:T(8,128)(2,1)S(1)} %fusion.2.refs_0_), channel_id=1, source_target_pairs={{0,2},{1,3},{2,4},{3,5},{4,6},{5,7},{6,0},{7,1},{8,10},{9,11},{10,... | collective-permute-start | bytes 442376 | tf_op jit(solution)/shard_map/ppermute | solution.py:328
  87.4 8.1 %collective-permute-start.15 = (bf16[64,1152]{1,0:T(8,128)(2,1)S(1)}, bf16[64,1152]{1,0:T(8,128)(2,1)S(1)}, u32[]{:S(2)}, u32[]{:S(2)}) collective-permute-start(bf16[64,1152]{1,0:T(8,128)(2,1)S(1)} %fusion.2.refs_0_), channel_id=1, source_target_pairs={{0,6},{1,7},{2,0},{3,1},{4,2},{5,3},{6,4},{7,5},{8,14},{9,15},{10,... | collective-permute-start | bytes 442376 | tf_op jit(solution)/shard_map/ppermute | solution.py:328
  95.6 12.0 %collective-permute-start.17 = (bf16[128,1152]{1,0:T(8,128)(2,1)S(1)}, bf16[128,1152]{1,0:T(8,128)(2,1)S(1)}, u32[]{:S(2)}, u32[]{:S(2)}) collective-permute-start(bf16[128,1152]{1,0:T(8,128)(2,1)S(1)} %constant_dynamic-update-slice_fusion.2), channel_id=1, source_target_pairs={{0,1},{1,2},{2,3},{3,4},{4,5},{5,6},{6,7},{7,0},{8,9},{9,10},{10,1... | collective-permute-start | bytes 884744 | tf_op jit(solution)/shard_map/ppermute | solution.py:313
  97.7 10.8 %collective-permute-start.18 = (bf16[128,1152]{1,0:T(8,128)(2,1)S(1)}, bf16[128,1152]{1,0:T(8,128)(2,1)S(1)}, u32[]{:S(2)}, u32[]{:S(2)}) collective-permute-start(bf16[128,1152]{1,0:T(8,128)(2,1)S(1)} %constant_dynamic-update-slice_fusion.2), channel_id=1, source_target_pairs={{0,7},{1,0},{2,1},{3,2},{4,3},{5,4},{6,5},{7,6},{8,15},{9,8},{10,9... | collective-permute-start | bytes 884744 | tf_op jit(solution)/shard_map/ppermute | solution.py:313
  98.9 8.3 %collective-permute-start.16 = (bf16[64,1152]{1,0:T(8,128)(2,1)S(1)}, bf16[64,1152]{1,0:T(8,128)(2,1)S(1)}, u32[]{:S(2)}, u32[]{:S(2)}) collective-permute-start(bf16[64,1152]{1,0:T(8,128)(2,1)S(1)} %collective-permute-done.14.refs_1_), channel_id=1, source_target_pairs={{0,2},{1,3},{2,4},{3,5},{4,6},{5,7},{6,0},{7,1},{8,10},{9,11},{10,... | collective-permute-start | bytes 442376 | tf_op jit(solution)/shard_map/ppermute | solution.py:328
  112.3 7.7 %collective-permute-start.19 = (bf16[3,432,1152]{2,1,0:T(8,128)(2,1)S(1)}, bf16[3,432,1152]{2,1,0:T(8,128)(2,1)}, u32[]{:S(2)}, u32[]{:S(2)}) collective-permute-start(bf16[3,432,1152]{2,1,0:T(8,128)(2,1)S(1)} %shard_map.79.refs_2_), channel_id=1, source_target_pairs={{0,16},{16,0},{32,48},{48,32},{64,80},{80,64},{96,112},{112,96},{1... | collective-permute-start | bytes 8957960 | tf_op jit(solution)/shard_map/ppermute | solution.py:319
  113.3 1.2 slice-start
  127.2 14.9 %collective-permute-start.21 = (bf16[128,1152]{1,0:T(8,128)(2,1)S(1)}, bf16[128,1152]{1,0:T(8,128)(2,1)S(1)}, u32[]{:S(2)}, u32[]{:S(2)}) collective-permute-start(bf16[128,1152]{1,0:T(8,128)(2,1)S(1)} %get-tuple-element.49), channel_id=1, source_target_pairs={{0,1},{1,2},{2,3},{3,4},{4,5},{5,6},{6,7},{7,0},{8,9},{9,10},{10,1... | collective-permute-start | bytes 884744 | tf_op jit(solution)/shard_map/ppermute | solution.py:313
  128.5 13.6 %collective-permute-start.20 = (bf16[128,1152]{1,0:T(8,128)(2,1)S(1)}, bf16[128,1152]{1,0:T(8,128)(2,1)S(1)}, u32[]{:S(2)}, u32[]{:S(2)}) collective-permute-start(bf16[128,1152]{1,0:T(8,128)(2,1)S(1)} %get-tuple-element.48), channel_id=1, source_target_pairs={{0,7},{1,0},{2,1},{3,2},{4,3},{5,4},{6,5},{7,6},{8,15},{9,8},{10,9... | collective-permute-start | bytes 884744 | tf_op jit(solution)/shard_map/ppermute | solution.py:313
  130.5 11.6 %collective-permute-start.22 = (bf16[64,1152]{1,0:T(8,128)(2,1)S(1)}, bf16[64,1152]{1,0:T(8,128)(2,1)S(1)}, u32[]{:S(2)}, u32[]{:S(2)}) collective-permute-start(bf16[64,1152]{1,0:T(8,128)(2,1)S(1)} %get-tuple-element.50), channel_id=1, source_target_pairs={{0,6},{1,7},{2,0},{3,1},{4,2},{5,3},{6,4},{7,5},{8,14},{9,15},{10,... | collective-permute-start | bytes 442376 | tf_op jit(solution)/shard_map/ppermute | solution.py:328
  142.2 11.1 %collective-permute-start.24 = (bf16[64,1152]{1,0:T(8,128)(2,1)S(1)}, bf16[64,1152]{1,0:T(8,128)(2,1)S(1)}, u32[]{:S(2)}, u32[]{:S(2)}) collective-permute-start(bf16[64,1152]{1,0:T(8,128)(2,1)S(1)} %get-tuple-element.66), channel_id=1, source_target_pairs={{0,2},{1,3},{2,4},{3,5},{4,6},{5,7},{6,0},{7,1},{8,10},{9,11},{10,... | collective-permute-start | bytes 442376 | tf_op jit(solution)/shard_map/ppermute | solution.py:328
  144.1 9.2 %collective-permute-start.23 = (bf16[64,1152]{1,0:T(8,128)(2,1)S(1)}, bf16[64,1152]{1,0:T(8,128)(2,1)S(1)}, u32[]{:S(2)}, u32[]{:S(2)}) collective-permute-start(bf16[64,1152]{1,0:T(8,128)(2,1)S(1)} %get-tuple-element.65), channel_id=1, source_target_pairs={{0,6},{1,7},{2,0},{3,1},{4,2},{5,3},{6,4},{7,5},{8,14},{9,15},{10,... | collective-permute-start | bytes 442376 | tf_op jit(solution)/shard_map/ppermute | solution.py:328
  146.5 37.2 %collective-permute-start.33 = (bf16[336,1152]{1,0:T(8,128)(2,1)S(1)}, bf16[336,1152]{1,0:T(8,128)(2,1)S(1)}, u32[]{:S(2)}, u32[]{:S(2)}) collective-permute-start(bf16[336,1152]{1,0:T(8,128)(2,1)S(1)} %get-tuple-element.52), channel_id=1, source_target_pairs={{0,32},{16,48},{32,0},{48,16},{64,96},{80,112},{96,64},{112,80},{1... | collective-permute-start | bytes 2322440 | tf_op jit(solution)/shard_map/ppermute | solution.py:319
  149.6 34.0 %collective-permute-start.34 = (bf16[336,1152]{1,0:T(8,128)(2,1)S(1)}, bf16[336,1152]{1,0:T(8,128)(2,1)S(1)}, u32[]{:S(2)}, u32[]{:S(2)}) collective-permute-start(bf16[336,1152]{1,0:T(8,128)(2,1)S(1)} %get-tuple-element.53), channel_id=1, source_target_pairs={{0,32},{16,48},{32,0},{48,16},{64,96},{80,112},{96,64},{112,80},{1... | collective-permute-start | bytes 2322440 | tf_op jit(solution)/shard_map/ppermute | solution.py:319
  153.4 30.2 %collective-permute-start.25 = (bf16[64,1152]{1,0:T(8,128)(2,1)S(1)}, bf16[64,1152]{1,0:T(8,128)(2,1)S(1)}, u32[]{:S(2)}, u32[]{:S(2)}) collective-permute-start(bf16[64,1152]{1,0:T(8,128)(2,1)S(1)} %fusion.7), channel_id=1, source_target_pairs={{0,8},{1,9},{2,10},{3,11},{4,12},{5,13},{6,14},{7,15},{8,0},{9,1},... | collective-permute-start | bytes 442376 | tf_op jit(solution)/shard_map/ppermute | solution.py:316
  183.8 44.3 %collective-permute-start.35 = (bf16[672,1152]{1,0:T(8,128)(2,1)S(1)}, bf16[672,1152]{1,0:T(8,128)(2,1)S(1)}, u32[]{:S(2)}, u32[]{:S(2)}) collective-permute-start(bf16[672,1152]{1,0:T(8,128)(2,1)S(1)} %shard_map.81.direct), channel_id=1, source_target_pairs={{0,16},{16,0},{32,48},{48,32},{64,80},{80,64},{96,112},{112,96},{1... | collective-permute-start | bytes 4644872 | tf_op jit(solution)/shard_map/ppermute | solution.py:319
  184.2 7.8 %collective-permute-start.26 = (bf16[64,1152]{1,0:T(8,128)(2,1)S(1)}, bf16[64,1152]{1,0:T(8,128)(2,1)S(1)}, u32[]{:S(2)}, u32[]{:S(2)}) collective-permute-start(bf16[64,1152]{1,0:T(8,128)(2,1)S(1)} %fusion.5.refs_0_), channel_id=1, source_target_pairs={{0,32},{16,48},{32,0},{48,16},{64,96},{80,112},{96,64},{112,80},{1... | collective-permute-start | bytes 442376 | tf_op jit(solution)/shard_map/ppermute | solution.py:319
  186.2 8.6 %collective-permute-start.36 = (bf16[64,1152]{1,0:T(8,128)(2,1)S(1)}, bf16[64,1152]{1,0:T(8,128)(2,1)S(1)}, u32[]{:S(2)}, u32[]{:S(2)}) collective-permute-start(bf16[64,1152]{1,0:T(8,128)(2,1)S(1)} %fusion.5.refs_0_), channel_id=1, source_target_pairs={{0,2},{1,3},{2,4},{3,5},{4,6},{5,7},{6,0},{7,1},{8,10},{9,11},{10,... | collective-permute-start | bytes 442376 | tf_op jit(solution)/shard_map/ppermute | solution.py:328
  188.4 39.8 %collective-permute-start.32 = (bf16[512,1152]{1,0:T(8,128)(2,1)S(1)}, bf16[512,1152]{1,0:T(8,128)(2,1)S(1)}, u32[]{:S(2)}, u32[]{:S(2)}) collective-permute-start(bf16[512,1152]{1,0:T(8,128)(2,1)S(1)} %pad_maximum_fusion.refs_4_.refs_6_), channel_id=1, source_target_pairs={{0,32},{16,48},{32,0},{48,16},{64,96},{80,112},{96,64},{112,80},{1... | collective-permute-start | bytes 3538952 | tf_op jit(solution)/shard_map/ppermute | solution.py:319
  190.1 8.7 %collective-permute-start.37 = (bf16[64,1152]{1,0:T(8,128)(2,1)S(1)}, bf16[64,1152]{1,0:T(8,128)(2,1)S(1)}, u32[]{:S(2)}, u32[]{:S(2)}) collective-permute-start(bf16[64,1152]{1,0:T(8,128)(2,1)S(1)} %fusion.5.refs_0_), channel_id=1, source_target_pairs={{0,6},{1,7},{2,0},{3,1},{4,2},{5,3},{6,4},{7,5},{8,14},{9,15},{10,... | collective-permute-start | bytes 442376 | tf_op jit(solution)/shard_map/ppermute | solution.py:328
  192.1 11.2 %collective-permute-start.27 = (bf16[64,1152]{1,0:T(8,128)(2,1)S(1)}, bf16[64,1152]{1,0:T(8,128)(2,1)S(1)}, u32[]{:S(2)}, u32[]{:S(2)}) collective-permute-start(bf16[64,1152]{1,0:T(8,128)(2,1)S(1)} %collective-permute-done.26.refs_0_), channel_id=1, source_target_pairs={{0,2},{1,3},{2,4},{3,5},{4,6},{5,7},{6,0},{7,1},{8,10},{9,11},{10,... | collective-permute-start | bytes 442376 | tf_op jit(solution)/shard_map/ppermute | solution.py:328
  198.8 24.0 %collective-permute-start.39 = (bf16[128,1152]{1,0:T(8,128)(2,1)S(1)}, bf16[128,1152]{1,0:T(8,128)(2,1)S(1)}, u32[]{:S(2)}, u32[]{:S(2)}) collective-permute-start(bf16[128,1152]{1,0:T(8,128)(2,1)S(1)} %constant_dynamic-update-slice_fusion.6), channel_id=1, source_target_pairs={{0,1},{1,2},{2,3},{3,4},{4,5},{5,6},{6,7},{7,0},{8,9},{9,10},{10,1... | collective-permute-start | bytes 884744 | tf_op jit(solution)/shard_map/ppermute | solution.py:313
  202.4 21.8 %collective-permute-start.40 = (bf16[128,1152]{1,0:T(8,128)(2,1)S(1)}, bf16[128,1152]{1,0:T(8,128)(2,1)S(1)}, u32[]{:S(2)}, u32[]{:S(2)}) collective-permute-start(bf16[128,1152]{1,0:T(8,128)(2,1)S(1)} %constant_dynamic-update-slice_fusion.6), channel_id=1, source_target_pairs={{0,7},{1,0},{2,1},{3,2},{4,3},{5,4},{6,5},{7,6},{8,15},{9,8},{10,9... | collective-permute-start | bytes 884744 | tf_op jit(solution)/shard_map/ppermute | solution.py:313
  203.3 9.2 %collective-permute-start.28 = (bf16[64,1152]{1,0:T(8,128)(2,1)S(1)}, bf16[64,1152]{1,0:T(8,128)(2,1)S(1)}, u32[]{:S(2)}, u32[]{:S(2)}) collective-permute-start(bf16[64,1152]{1,0:T(8,128)(2,1)S(1)} %collective-permute-done.26.refs_0_), channel_id=1, source_target_pairs={{0,6},{1,7},{2,0},{3,1},{4,2},{5,3},{6,4},{7,5},{8,14},{9,15},{10,... | collective-permute-start | bytes 442376 | tf_op jit(solution)/shard_map/ppermute | solution.py:328
  212.5 7.4 %collective-permute-start.38 = (bf16[64,1152]{1,0:T(8,128)(2,1)S(1)}, bf16[64,1152]{1,0:T(8,128)(2,1)S(1)}, u32[]{:S(2)}, u32[]{:S(2)}) collective-permute-start(bf16[64,1152]{1,0:T(8,128)(2,1)S(1)} %collective-permute-done.36.refs_1_), channel_id=1, source_target_pairs={{0,2},{1,3},{2,4},{3,5},{4,6},{5,7},{6,0},{7,1},{8,10},{9,11},{10,... | collective-permute-start | bytes 442376 | tf_op jit(solution)/shard_map/ppermute | solution.py:328
  219.8 13.7 %collective-permute-start.30 = (bf16[128,1152]{1,0:T(8,128)(2,1)S(1)}, bf16[128,1152]{1,0:T(8,128)(2,1)S(1)}, u32[]{:S(2)}, u32[]{:S(2)}) collective-permute-start(bf16[128,1152]{1,0:T(8,128)(2,1)S(1)} %constant_dynamic-update-slice_fusion.4), channel_id=1, source_target_pairs={{0,1},{1,2},{2,3},{3,4},{4,5},{5,6},{6,7},{7,0},{8,9},{9,10},{10,1... | collective-permute-start | bytes 884744 | tf_op jit(solution)/shard_map/ppermute | solution.py:313
  222.8 10.8 %collective-permute-start.31 = (bf16[128,1152]{1,0:T(8,128)(2,1)S(1)}, bf16[128,1152]{1,0:T(8,128)(2,1)S(1)}, u32[]{:S(2)}, u32[]{:S(2)}) collective-permute-start(bf16[128,1152]{1,0:T(8,128)(2,1)S(1)} %constant_dynamic-update-slice_fusion.4), channel_id=1, source_target_pairs={{0,7},{1,0},{2,1},{3,2},{4,3},{5,4},{6,5},{7,6},{8,15},{9,8},{10,9... | collective-permute-start | bytes 884744 | tf_op jit(solution)/shard_map/ppermute | solution.py:313
  224.3 9.3 %collective-permute-start.29 = (bf16[64,1152]{1,0:T(8,128)(2,1)S(1)}, bf16[64,1152]{1,0:T(8,128)(2,1)S(1)}, u32[]{:S(2)}, u32[]{:S(2)}) collective-permute-start(bf16[64,1152]{1,0:T(8,128)(2,1)S(1)} %collective-permute-done.27.refs_1_), channel_id=1, source_target_pairs={{0,2},{1,3},{2,4},{3,5},{4,6},{5,7},{6,0},{7,1},{8,10},{9,11},{10,... | collective-permute-start | bytes 442376 | tf_op jit(solution)/shard_map/ppermute | solution.py:328
